TPU v7x, 32 devices: a whole 2x2x4 slice. The times are simulated.
32 devices in a mesh: cx: 8 (over z, x), cy: 4 (over y, core).
Axes of the slice: x: 2, y: 2, z: 4, core: 2. Of those that a mesh axis runs over, the one named last changes fastest.
Arguments:
- cell_pos: float32 [32, 16, 3, 1024], P('cx', 'cy'), may hold values from -6 to 6
- cell_drag: float32 [32, 16], P('cx', 'cy'), may hold values from 0.2 to 2
- cell_near: int32 [32, 16, 2], P('cx', 'cy'), may hold values from 0 to 511, as said below
- analysis: bfloat16 [1024, 1024], replicated, may hold values from -0.1875 to 0.1875
- stiffness: float32 [1024], replicated, may hold values from 0.1 to 1
- synthesis: bfloat16 [1024, 1024], replicated, may hold values from -0.1875 to 0.1875
- wall_pos: float32 [256, 3, 256], P(('cx', 'cy')), may hold values from -9 to 9
- wall_normal: float32 [256, 3, 256], P(('cx', 'cy')), may hold values from -6 to 6
- wall_weight: float32 [256, 256], P(('cx', 'cy')), may hold values from 0.02 to 0.2
- density: float32 [256, 3, 256], P(('cx', 'cy')), may hold values from -6 to 6
- patch_near: int32 [256, 4], P(('cx', 'cy')), may hold values from 0 to 255, as said below
- cell_to_patch: int32 [256, 2], P(('cx', 'cy')), may hold values from 0 to 511, as said below
Outputs:
- moved_cells: float32 [32, 16, 3, 1024], P('cx', 'cy')
- density_next: float32 [256, 3, 256], P(('cx', 'cy'))
Inputs may be any that keep to these rules, and one draw needn't show every extreme that they name: `cell_near`: each entry is the row-major index (row times 16 plus column) of a cell whose grid row and column differ from the listing cell's by at most 3 each, cyclically, and never the listing cell itself. `cell_to_patch`: for the patches of block b (patches b * 8 to b * 8 + 7), with b = i * 4 + j, each entry is the row-major index of a cell whose row lies within 3 of the rows i * 4 to i * 4 + 3 and whose column lies within 3 of the columns j * 4 to j * 4 + 3, cyclically. `patch_near`: each entry is a patch of the listing patch's block of 8 or of the two blocks beside it, cyclically, and never the listing patch itself.
All inputs are finite; a program needn't handle non-finite values.
Results may differ from a plain program's by a relative error of at most 0.0041.
Values sent between devices are 32-bit elements; how exact they have to be, the bound alone decides.
A program may use at most 64 MiB of HBM per device.

v0:
```python
import functools
import math

import jax
import jax.numpy as jnp
from jax import lax
from jax.experimental import pallas as pl
from jax.experimental.pallas import tpu as pltpu
from jax.sharding import PartitionSpec as P

HALO = 3
WIDTH = 512

soften = 0.25
stokes_scale = 1.0 / (8.0 * math.pi)
layer_scale = 3.0 / (4.0 * math.pi)

MESH = pl.DeviceIdType.MESH
f32 = jnp.float32
bf16 = jnp.bfloat16


def halo_kernel(size_x, size_y, cell_ref, wall_ref, ext_ref, walls_ref, send, recv, local):
    me_x, me_y = lax.axis_index("cx"), lax.axis_index("cy")
    rows, cols = cell_ref.shape[0], cell_ref.shape[1]
    patches = wall_ref.shape[0]

    def side(step, length):
        if step == 1:
            return slice(length - HALO, length), slice(0, HALO)
        if step == 0:
            return slice(0, length), slice(HALO, HALO + length)
        return slice(0, HALO), slice(HALO + length, 2 * HALO + length)

    pieces_out = []
    for dx in (0, 1, -1):
        for dy in (1, -1, 0):
            if dx == 0 and dy == 0:
                continue
            device = (lax.rem(me_x + dx + size_x, size_x), lax.rem(me_y + dy + size_y, size_y))
            (take_x, put_x), (take_y, put_y) = side(dx, rows), side(dy, cols)
            pieces_out.append((cell_ref.at[take_x, take_y], ext_ref.at[put_x, put_y], device))
    flat = me_x * size_y + me_y
    for step, first in ((1, 0), (-1, 2 * patches)):
        other = lax.rem(flat + step + size_x * size_y, size_x * size_y)
        device = (other // size_y, lax.rem(other, size_y))
        pieces_out.append((wall_ref, walls_ref.at[first : first + patches], device))

    barrier = pltpu.get_barrier_semaphore()
    for _, _, device in pieces_out:
        pl.semaphore_signal(barrier, inc=1, device_id=device, device_id_type=MESH)
    pl.semaphore_wait(barrier, len(pieces_out))
    copies = []
    for k, (src, dst, device) in enumerate(pieces_out):
        copy = pltpu.make_async_remote_copy(
            src_ref=src,
            dst_ref=dst,
            send_sem=send.at[k],
            recv_sem=recv.at[k],
            device_id=device,
            device_id_type=MESH,
        )
        copy.start()
        copies.append(copy)
    own = ext_ref.at[HALO : HALO + rows, HALO : HALO + cols]
    copies.append(pltpu.make_async_copy(cell_ref, own, local.at[0]))
    copies[-1].start()
    copies.append(pltpu.make_async_copy(wall_ref, walls_ref.at[patches : 2 * patches], local.at[1]))
    copies[-1].start()
    for copy in copies:
        copy.wait()


def halos(cells, walls, size_x, size_y):
    rows, cols, _, points = cells.shape
    dma = pltpu.SemaphoreType.DMA
    return pl.pallas_call(
        functools.partial(halo_kernel, size_x, size_y),
        out_shape=(
            jax.ShapeDtypeStruct((rows + 2 * HALO, cols + 2 * HALO, 3, points), f32),
            jax.ShapeDtypeStruct((3 * walls.shape[0], *walls.shape[1:]), f32),
        ),
        in_specs=[pl.BlockSpec(memory_space=pltpu.VMEM)] * 2,
        out_specs=[pl.BlockSpec(memory_space=pl.ANY)] * 2,
        scratch_shapes=[dma((10,)), dma((10,)), dma((2,))],
        compiler_params=pltpu.CompilerParams(collective_id=1, has_side_effects=True),
        name="halos",
    )(cells, walls)


def membrane_kernel(pos_ref, analysis_ref, stiffness_ref, synthesis_ref, out_ref, flat_ref):
    count = pos_ref.shape[0]
    for c in range(count):
        flat_ref[3 * c : 3 * c + 3, :] = pos_ref[c]
    value = flat_ref[0 : 3 * count, :]
    centred = (value - jnp.mean(value, axis=1, keepdims=True)).astype(bf16)
    coeff = jnp.dot(centred, analysis_ref[...], preferred_element_type=f32)
    scaled = (coeff * stiffness_ref[...]).astype(bf16)
    flat_ref[0 : 3 * count, :] = -jnp.dot(scaled, synthesis_ref[...], preferred_element_type=f32)
    for c in range(count):
        out_ref[c] = flat_ref[3 * c : 3 * c + 3, :]


def membrane(positions, analysis, stiffness, synthesis):
    count, _, points = positions.shape
    return pl.pallas_call(
        membrane_kernel,
        out_shape=jax.ShapeDtypeStruct(positions.shape, f32),
        in_specs=[pl.BlockSpec(memory_space=pltpu.VMEM)] * 4,
        out_specs=pl.BlockSpec(memory_space=pltpu.VMEM),
        scratch_shapes=[pltpu.VMEM((-(-3 * count // 8) * 8, points), f32)],
        name="membrane",
    )(positions, analysis, stiffness[None, :], synthesis)


def local_slot(global_id, first_row, first_col, all_rows, all_cols, ext_cols):
    grid_row = global_id // all_cols
    grid_col = global_id % all_cols
    local_row = (grid_row - first_row + HALO) % all_rows
    local_col = (grid_col - first_col + HALO) % all_cols
    return local_row * ext_cols + local_col


def pieces(value):
    high = value.astype(bf16).astype(f32)
    rest = value - high
    middle = rest.astype(bf16).astype(f32)
    return high, middle, rest - middle


def rows8(points):
    return [jnp.broadcast_to(points[i : i + 1, :], (8, points.shape[1])) for i in range(3)]


def pick(row, values):
    out = jnp.zeros_like(values[0])
    for i, value in enumerate(values):
        out = jnp.where(row == i, value, out)
    return out


def target_features(points):
    x0, x1, x2 = rows8(points)
    row = lax.broadcasted_iota(jnp.int32, x0.shape, 0)
    square = x0 * x0 + x1 * x1 + x2 * x2
    high, middle, low = pieces(pick(row, [x0, x1, x2, square, jnp.ones_like(x0)]))
    return jnp.concatenate([high, high, middle, high, low, middle], axis=0).astype(bf16)


def source_side(value):
    high, middle, low = pieces(value)
    stacked = jnp.concatenate([high, middle, high, low, high, middle], axis=0)
    return stacked.T.astype(bf16)


def distance_features(y, row):
    y0, y1, y2 = y
    square = y0 * y0 + y1 * y1 + y2 * y2 + soften
    return source_side(pick(row, [-2.0 * y0, -2.0 * y1, -2.0 * y2, jnp.ones_like(y0), square]))


def stokes_prepare(source, force, side_ref, coef_ref, base):
    y = rows8(source)
    f = rows8(force)
    row = lax.broadcasted_iota(jnp.int32, y[0].shape, 0)
    along = y[0] * f[0] + y[1] * f[1] + y[2] * f[2]
    square = y[0] * y[0] + y[1] * y[1] + y[2] * y[2]
    f8 = pick(row % 4, [f[0], f[1], f[2], along])
    h1, m1, l1 = pieces(f8 * jnp.where(row < 4, 1.0, y[0]))
    h2, m2, l2 = pieces(f8 * jnp.where(row < 4, y[1], y[2]))
    h3, m3, l3 = pieces(f8 * square)
    points = source.shape[1]
    side_ref[base : base + points] = distance_features(y, row)
    coef_ref[:, base : base + points] = jnp.concatenate(
        [h1, h2, h3, m1, m2, m3, l1, l2, l3], axis=0
    ).astype(bf16)


def stokes_sums(features, side_ref, coef_ref, acc_ref, width):
    side = side_ref[...]
    coef = coef_ref[...]
    for t in range(features.shape[1] // width):
        part = slice(t * width, (t + 1) * width)
        root = lax.rsqrt(jnp.dot(side, features[:, part], preferred_element_type=f32))
        cube = (root * root * root).astype(bf16)
        acc_ref[:, part] = jnp.dot(coef, cube, preferred_element_type=f32)


def stokes_finish(target, acc_ref):
    x = [target[i : i + 1, :] for i in range(3)]
    low = acc_ref[0:8, :] + (acc_ref[24:32, :] + acc_ref[48:56, :])
    high = acc_ref[8:16, :] + (acc_ref[32:40, :] + acc_ref[56:64, :])
    far = acc_ref[16:24, :] + (acc_ref[40:48, :] + acc_ref[64:72, :])
    square = x[0] * x[0] + x[1] * x[1] + x[2] * x[2] + 2.0 * soften

    def contract(block, at):
        out = -block[at + 3 : at + 4]
        for j in range(3):
            out = out + x[j] * block[at + j : at + j + 1]
        return out

    line = contract(low, 0)
    turned = [contract(low, 4), contract(high, 0), contract(high, 4)]
    out = []
    for i in range(3):
        cross = x[0] * low[4 + i : 5 + i] + x[1] * high[i : i + 1] + x[2] * high[4 + i : 5 + i]
        direct = square * low[i : i + 1] + far[i : i + 1] - 2.0 * cross
        out.append(stokes_scale * (direct + x[i] * line - turned[i]))
    return out


def cell_kernel(
    slot_ref, own_ref, drag_ref, target_ref, pos_ref, force_ref, out_ref, top_ref,
    side_ref, coef_ref, acc_ref, *, near
):
    cell = pl.program_id(0)
    target = target_ref[0]
    per_cell = pos_ref.shape[2]
    features = target_features(target)
    for n in range(near):
        slot = slot_ref[cell, n]
        stokes_prepare(pos_ref[slot], force_ref[slot], side_ref, coef_ref, n * per_cell)
    stokes_sums(features, side_ref, coef_ref, acc_ref, min(WIDTH, target.shape[1]))
    own = force_ref[own_ref[cell]]
    drag = drag_ref[cell]
    parts = stokes_finish(target, acc_ref)
    square = jnp.zeros_like(parts[0])
    for i in range(3):
        value = drag * own[i : i + 1] + parts[i]
        out_ref[0, i : i + 1, :] = value
        square = square + value * value
    best = jnp.broadcast_to(jnp.max(square, axis=1, keepdims=True), (1, 128))

    @pl.when(cell == 0)
    def _():
        top_ref[...] = best

    @pl.when(cell > 0)
    def _():
        top_ref[...] = jnp.maximum(top_ref[...], best)


def cell_velocity(cells, drag, near_slots, own_slots, flat_pos, flat_force):
    count, _, points = cells.shape
    near = near_slots.shape[1]
    sources = near * points
    whole = pl.BlockSpec(flat_pos.shape, lambda i, *_: (0, 0, 0), pipeline_mode=pl.Buffered(1))
    one = pl.BlockSpec((1, 3, points), lambda i, *_: (i, 0, 0))
    return pl.pallas_call(
        functools.partial(cell_kernel, near=near),
        grid_spec=pltpu.PrefetchScalarGridSpec(
            num_scalar_prefetch=3,
            grid=(count,),
            in_specs=[one, whole, whole],
            out_specs=[one, pl.BlockSpec((1, 128), lambda i, *_: (0, 0))],
            scratch_shapes=[
                pltpu.VMEM((sources, 48), bf16),
                pltpu.VMEM((72, sources), bf16),
                pltpu.VMEM((72, points), f32),
            ],
        ),
        out_shape=(
            jax.ShapeDtypeStruct(cells.shape, f32),
            jax.ShapeDtypeStruct((1, 128), f32),
        ),
        name="cell_velocity",
    )(near_slots, own_slots, drag, cells, flat_pos, flat_force)


def wall_kernel(
    cell_slot_ref, patch_slot_ref, target_ref, pos_ref, force_ref, wall_ref, out_ref,
    side_ref, coef_ref, acc_ref, layer_ref, moment_ref, *, near, listed
):
    patch = pl.program_id(0)
    target = target_ref[0]
    points = target.shape[1]
    per_cell = pos_ref.shape[2]
    features = target_features(target)
    for n in range(near):
        slot = cell_slot_ref[patch, n]
        stokes_prepare(pos_ref[slot], force_ref[slot], side_ref, coef_ref, n * per_cell)
    stokes_sums(features, side_ref, coef_ref, acc_ref, min(WIDTH, points))
    flow = stokes_finish(target, acc_ref)
    for n in range(listed):
        source = wall_ref[patch_slot_ref[patch, n]]
        y = rows8(source[0:3])
        normal = rows8(source[3:6])
        value = rows8(source[6:9])
        weight = -layer_scale * jnp.broadcast_to(source[9:10], y[0].shape)
        value = [weight * v for v in value]
        row = lax.broadcasted_iota(jnp.int32, y[0].shape, 0)
        zero = jnp.zeros_like(y[0])

        def linear(v):
            return source_side(pick(row, [*v, zero, -(y[0] * v[0] + y[1] * v[1] + y[2] * v[2])]))

        part = slice(n * points, (n + 1) * points)
        layer_ref[0, part] = distance_features(y, row)
        layer_ref[1, part] = linear(value)
        layer_ref[2, part] = linear(normal)
        high, middle, low = pieces(pick(row, [*y, jnp.ones_like(y[0])]))
        moment_ref[:, part] = jnp.concatenate([high, middle, low, zero], axis=0).astype(bf16)
    root = lax.rsqrt(jnp.dot(layer_ref[0], features, preferred_element_type=f32))
    along_q = jnp.dot(layer_ref[1], features, preferred_element_type=f32)
    along_n = jnp.dot(layer_ref[2], features, preferred_element_type=f32)
    square = root * root
    scalar = (along_q * along_n * (square * square * root)).astype(bf16)
    total = jnp.dot(moment_ref[...], scalar, preferred_element_type=f32)
    moment = total[0:8] + (total[8:16] + total[16:24])
    for i in range(3):
        layer = target[i : i + 1] * moment[3:4] - moment[i : i + 1]
        out_ref[0, i : i + 1, :] = 2.0 * layer + 2.0 * flow[i]


def wall_density(wall_pos, cell_slots, patch_slots, flat_pos, flat_force, ext_wall):
    count, _, points = wall_pos.shape
    near, listed = cell_slots.shape[1], patch_slots.shape[1]
    sources = near * flat_pos.shape[2]
    whole = pl.BlockSpec(flat_pos.shape, lambda i, *_: (0, 0, 0), pipeline_mode=pl.Buffered(1))
    walls = pl.BlockSpec(ext_wall.shape, lambda i, *_: (0, 0, 0), pipeline_mode=pl.Buffered(1))
    one = pl.BlockSpec((1, 3, points), lambda i, *_: (i, 0, 0))
    return pl.pallas_call(
        functools.partial(wall_kernel, near=near, listed=listed),
        grid_spec=pltpu.PrefetchScalarGridSpec(
            num_scalar_prefetch=2,
            grid=(count,),
            in_specs=[one, whole, whole, walls],
            out_specs=one,
            scratch_shapes=[
                pltpu.VMEM((sources, 48), bf16),
                pltpu.VMEM((72, sources), bf16),
                pltpu.VMEM((72, points), f32),
                pltpu.VMEM((3, listed * points, 48), bf16),
                pltpu.VMEM((32, listed * points), bf16),
            ],
        ),
        out_shape=jax.ShapeDtypeStruct(wall_pos.shape, f32),
        name="wall_density",
    )(cell_slots, patch_slots, wall_pos, flat_pos, flat_force, ext_wall)


def top_kernel(size_x, size_y, mine_ref, out_ref, row_ref, from_y, from_x, send_y, recv_y, send_x, recv_x):
    me_x, me_y = lax.axis_index("cx"), lax.axis_index("cy")
    barrier = pltpu.get_barrier_semaphore()
    for d in range(1, size_y):
        pl.semaphore_signal(
            barrier, inc=1, device_id=(me_x, lax.rem(me_y + d, size_y)), device_id_type=MESH
        )
    for d in range(1, size_x):
        pl.semaphore_signal(
            barrier, inc=1, device_id=(lax.rem(me_x + d, size_x), me_y), device_id_type=MESH
        )
    pl.semaphore_wait(barrier, size_x + size_y - 2)
    copies = []
    for d in range(1, size_y):
        copy = pltpu.make_async_remote_copy(
            src_ref=mine_ref,
            dst_ref=from_y.at[d - 1],
            send_sem=send_y.at[d - 1],
            recv_sem=recv_y.at[d - 1],
            device_id=(me_x, lax.rem(me_y + d, size_y)),
            device_id_type=MESH,
        )
        copy.start()
        copies.append(copy)
    best = mine_ref[...]
    for d, copy in enumerate(copies):
        copy.wait()
        best = jnp.maximum(best, from_y[d])
    row_ref[...] = best
    copies = []
    for d in range(1, size_x):
        copy = pltpu.make_async_remote_copy(
            src_ref=row_ref,
            dst_ref=from_x.at[d - 1],
            send_sem=send_x.at[d - 1],
            recv_sem=recv_x.at[d - 1],
            device_id=(lax.rem(me_x + d, size_x), me_y),
            device_id_type=MESH,
        )
        copy.start()
        copies.append(copy)
    for d, copy in enumerate(copies):
        copy.wait()
        best = jnp.maximum(best, from_x[d])
    out_ref[...] = best


def top_of_all(mine, size_x, size_y):
    dma = pltpu.SemaphoreType.DMA
    return pl.pallas_call(
        functools.partial(top_kernel, size_x, size_y),
        out_shape=jax.ShapeDtypeStruct(mine.shape, f32),
        in_specs=[pl.BlockSpec(memory_space=pltpu.VMEM)],
        out_specs=pl.BlockSpec(memory_space=pltpu.VMEM),
        scratch_shapes=[
            pltpu.VMEM(mine.shape, f32),
            pltpu.VMEM((size_y - 1, *mine.shape), f32),
            pltpu.VMEM((size_x - 1, *mine.shape), f32),
            dma((size_y - 1,)),
            dma((size_y - 1,)),
            dma((size_x - 1,)),
            dma((size_x - 1,)),
        ],
        compiler_params=pltpu.CompilerParams(collective_id=0, has_side_effects=True),
        name="top_of_all",
    )(mine)


def body(
    cell_pos,
    cell_drag,
    cell_near,
    analysis,
    stiffness,
    synthesis,
    wall_pos,
    wall_normal,
    wall_weight,
    density,
    patch_near,
    cell_to_patch,
):
    row_count = cell_pos.shape[0]
    col_count = cell_pos.shape[1]
    points = cell_pos.shape[3]
    ext_cols = col_count + 2 * HALO
    all_rows = row_count * lax.axis_size("cx")
    all_cols = col_count * lax.axis_size("cy")
    first_row = lax.axis_index("cx") * row_count
    first_col = lax.axis_index("cy") * col_count
    slot = functools.partial(
        local_slot,
        first_row=first_row,
        first_col=first_col,
        all_rows=all_rows,
        all_cols=all_cols,
        ext_cols=ext_cols,
    )
    packed = jnp.concatenate([wall_pos, wall_normal, density, wall_weight[:, None, :]], axis=1)
    ext_pos, ext_wall = halos(cell_pos, packed, lax.axis_size("cx"), lax.axis_size("cy"))
    flat_pos = ext_pos.reshape(-1, 3, points)
    flat_force = membrane(flat_pos, analysis, stiffness, synthesis)
    count = row_count * col_count
    near_slots = slot(cell_near).reshape(count, -1)
    ids = jnp.arange(count, dtype=jnp.int32)
    own_slots = (ids // col_count + HALO) * ext_cols + ids % col_count + HALO
    velocity, top_square = cell_velocity(
        cell_pos.reshape(count, 3, points),
        cell_drag.reshape(count),
        near_slots,
        own_slots,
        flat_pos,
        flat_force,
    )
    top = jnp.sqrt(top_of_all(top_square, lax.axis_size("cx"), lax.axis_size("cy"))[0, 0])
    step = 1.0 / (top + 1e-06)
    moved_cells = cell_pos + step * velocity.reshape(cell_pos.shape)
    patch_count = wall_pos.shape[0]
    all_patches = patch_count * lax.axis_size(("cx", "cy"))
    block_start = lax.axis_index(("cx", "cy")) * patch_count
    own_patches = jnp.arange(patch_count, dtype=jnp.int32) + patch_count
    other_slots = (patch_near - block_start + patch_count) % all_patches
    chosen = jnp.concatenate([own_patches[:, None], other_slots], axis=1)
    density_next = wall_density(
        wall_pos, slot(cell_to_patch), chosen, flat_pos, flat_force, ext_wall
    )
    return (moved_cells, density_next)


def solution(mesh):
    placed = (
        P("cx", "cy", None, None),
        P("cx", "cy"),
        P("cx", "cy", None),
        P(),
        P(),
        P(),
        P(("cx", "cy"), None, None),
        P(("cx", "cy"), None, None),
        P(("cx", "cy"), None),
        P(("cx", "cy"), None, None),
        P(("cx", "cy"), None),
        P(("cx", "cy"), None),
    )
    return jax.shard_map(
        body,
        mesh=mesh,
        in_specs=placed,
        out_specs=(P("cx", "cy", None, None), P(("cx", "cy"), None, None)),
        check_vma=False,
    )
```

profile of v0, /device:TPU:0, one launch (start us, length us, event | category | flops | bytes accessed | tf_op | source)
XLA Modules:
  0.0 119.6 jit_solution(3476579996356549061)
XLA Ops:
  0.6 1.2 %reshape.32.drag_ref = f32[16]{0:T(128)} reshape(f32[4,4]{1,0:T(4,128)} %param.13) | data formatting | bytes 128 | tf_op jit(solution)/shard_map/reshape | solution.py:450
  1.9 0.5 fusion.16.own_ref
  2.4 0.7 fusion
  3.1 0.7 copy.29
  3.9 0.8 copy.26
  4.6 0.8 copy.22
  5.4 0.6 fusion.5.cell_slot_ref
  6.0 0.7 pad_add_fusion.patch_slot_ref
  6.7 0.7 broadcast_in_dim.7
  7.4 0.8 copy.16.target_ref
  8.1 0.0 copy-start.1
  8.1 0.8 copy.17
  8.9 0.8 copy.18
  9.7 0.7 pad_maximum_fusion.wall_ref
  10.4 1.8 %copy.15.cell_ref = f32[4,4,3,1024]{3,2,1,0:T(4,128)} copy(f32[4,4,3,1024]{3,1,2,0:T(4,128)} %param.12) | data formatting | bytes 393216 | tf_op args[0]
  12.1 29.1 %halos.1 = (f32[10,10,3,1024]{3,2,1,0:T(4,128)}, f32[24,10,256]{2,1,0:T(8,128)}) custom-call(f32[4,4,3,1024]{3,2,1,0:T(4,128)} %copy.15.cell_ref, f32[8,10,256]{2,1,0:T(8,128)} %pad_maximum_fusion.wall_ref), custom_call_target="tpu_custom_call" | custom-call | tf_op jit(solution)/shard_map/halos/pallas_call | solution.py:77
  41.2 5.9 %membrane.1.force_ref = f32[100,3,1024]{2,1,0:T(4,128)} custom-call(f32[100,3,1024]{2,1,0:T(4,128)} %bitcast.7, bf16[1024,1024]{1,0:T(8,128)(2,1)} %analysis_ref.1, f32[1,1024]{1,0:T(1,128)} %bitcast.13, bf16[1024,1024]{1,0:T(8,128)(2,1)} %synthesis_ref.1), custom_call_target="tpu_custom_call" | custom-call | tf_op jit(solution)/shard_map/membrane/pallas_call | solution.py:106
  47.2 0.0 copy-done.1
  47.2 17.6 %wall_density.1 = f32[8,3,256]{2,1,0:T(4,128)} custom-call(s32[8,2]{1,0:T(8,128)} %fusion.5.cell_slot_ref, s32[8,5]{1,0:T(8,128)} %pad_add_fusion.patch_slot_ref, f32[8,3,256]{2,1,0:T(4,128)} %copy-done.1, f32[100,3,1024]{2,1,0:T(4,128)} %bitcast.8, f32[100,3,1024]{2,1,0:T(4,128)} %membrane.1.force_ref, f32[24,10,256]{2,1,0:T(8,128)} %get-tuple-element.9.wall_ref), custom_call_target="tpu_custom_call" | custom-call | tf_op jit(solution)/shard_map/wall_density/pallas_call | solution.py:322
  64.8 0.0 copy-start.2
  64.8 0.0 copy-start
  64.8 40.5 %cell_velocity.1 = (f32[16,3,1024]{2,1,0:T(4,128)}, f32[1,128]{1,0:T(1,128)}) custom-call(s32[16,2]{1,0:T(8,128)} %bitcast.12, s32[16]{0:T(128)} %fusion.16.own_ref, f32[16]{0:T(128)} %reshape.32.drag_ref, f32[16,3,1024]{2,1,0:T(4,128)} %bitcast.10, f32[100,3,1024]{2,1,0:T(4,128)} %bitcast.9, f32[100,3,1024]{2,1,0:T(4,128)} %membrane.1.force_ref), custom_call_target="tpu_custom_call" | custom-call | tf_op jit(solution)/shard_map/cell_velocity/pallas_call | solution.py:249
  105.2 0.0 copy-done.2
  105.2 0.6 copy.28
  105.9 11.2 %top_of_all.1 = f32[1,128]{1,0:T(1,128)} custom-call(f32[1,128]{1,0:T(1,128)} %get-tuple-element.7.mine_ref), custom_call_target="tpu_custom_call" | custom-call | tf_op jit(solution)/shard_map/top_of_all/pallas_call | solution.py:391
  117.8 1.0 broadcast_multiply_fusion
  118.8 0.0 copy-done
  118.8 0.8 copy_add_fusion
  (2 shorter events, 0.0 us)
Async XLA Ops:
  8.1 39.0 %copy-start.1 = (f32[8,3,256]{2,1,0:T(4,128)}, f32[8,3,256]{2,1,0:T(4,128)S(1)}, u32[]{:S(2)}) copy-start(f32[8,3,256]{2,1,0:T(4,128)S(1)} %copy.16.target_ref) | copy-start | bytes 73732
  64.8 40.5 %copy-start.2 = (f32[8,3,256]{2,1,0:T(4,128)S(1)}, f32[8,3,256]{2,1,0:T(4,128)}, u32[]{:S(2)}) copy-start(f32[8,3,256]{2,1,0:T(4,128)} %wall_density.1) | copy-start | bytes 73732
  64.8 54.0 %copy-start = (f32[4,4,3,1024]{3,1,2,0:T(4,128)S(1)}, f32[4,4,3,1024]{3,1,2,0:T(4,128)}, u32[]{:S(2)}) copy-start(f32[4,4,3,1024]{3,1,2,0:T(4,128)} %param.12) | copy-start | bytes 589828
where the time goes:
time: 120 us
  Pallas kernels  104 us (87%)
  local copies, waits for them, and re-layouts  8.81 us (7%)
  other arithmetic  5.1 us (4%)
  between operations  1.4 us (1%)
    pallas_call x1, Pallas kernels, cell_velocity(): pl.pallas_call(functools.partial(cell_kernel, near=near), grid_spec=pltpu...  40.5 us
    pallas_call x1, Pallas kernels, halos(): pl.pallas_call(functools.partial(halo_kernel, size_x, size_y), out_shape=...  29.1 us
    pallas_call x1, Pallas kernels, wall_density(): pl.pallas_call(functools.partial(wall_kernel, near=near, listed=listed),...  17.6 us
    pallas_call x1, Pallas kernels, top_of_all(): pl.pallas_call(functools.partial(top_kernel, size_x, size_y), out_shape=j...  11.2 us
    unnamed x13, local copies, waits for them, and re-layouts  6.16 us
    pallas_call x1, Pallas kernels, membrane(): pl.pallas_call(membrane_kernel, out_shape=jax.ShapeDtypeStruct(positions....  5.93 us

commit v1 on v0

v1 whole, which is shorter than its diff:
```python
import functools
import math

import jax
import jax.numpy as jnp
from jax import lax
from jax.experimental import pallas as pl
from jax.experimental.pallas import tpu as pltpu
from jax.sharding import PartitionSpec as P

HALO = 3
LANES = 128
WIDTH = 512

soften = 0.25
stokes_scale = 1.0 / (8.0 * math.pi)
layer_scale = 3.0 / (4.0 * math.pi)

MESH = pl.DeviceIdType.MESH
f32 = jnp.float32
bf16 = jnp.bfloat16


def pieces(value):
    high = value.astype(bf16).astype(f32)
    rest = value - high
    middle = rest.astype(bf16).astype(f32)
    return high, middle, rest - middle


def strided(ref, start, count, stride):
    return ref[pl.ds(start, count, stride=stride), :]


def put_wide(ref, first, value):
    tiles = value.shape[1] // LANES
    height = ref.shape[0] // tiles
    for k in range(tiles):
        at = k * height + first
        ref[at : at + value.shape[0], :] = value[:, k * LANES : (k + 1) * LANES]


def get_tile(ref, tiles, tile, start, count, stride):
    height = ref.shape[0] // tiles
    return ref[pl.ds(tile * height + start, count, stride=stride), :]


def get_wide(ref, tiles, start, count, stride):
    return jnp.concatenate([get_tile(ref, tiles, k, start, count, stride) for k in range(tiles)], axis=1)


class Shape:
    def __init__(self, rows, cols, points, size_x, size_y, near):
        self.rows, self.cols, self.points = rows, cols, points
        self.size_x, self.size_y, self.near = size_x, size_y, near
        self.ext_rows = rows + 2 * HALO
        self.sub = points // LANES
        self.cell = 3 * self.sub
        self.left = self.ext_rows * cols
        self.right = self.left + self.ext_rows * HALO
        self.slots = self.right + self.ext_rows * HALO


def cell_slot(shape, gid, me_x, me_y):
    all_rows, all_cols = shape.rows * shape.size_x, shape.cols * shape.size_y
    grid_row = lax.div(gid, jnp.int32(all_cols))
    grid_col = gid - grid_row * all_cols
    row = grid_row - me_x * shape.rows
    row = jnp.where(row < 0, row + all_rows, row)
    row = jnp.where(row >= shape.rows + HALO, row - all_rows + shape.ext_rows, row)
    col = grid_col - me_y * shape.cols + HALO
    col = jnp.where(col < 0, col + all_cols, col)
    col = jnp.where(col >= all_cols, col - all_cols, col)
    middle = row * shape.cols + col - HALO
    left = shape.left + row * HALO + col
    right = shape.right + row * HALO + col - HALO - shape.cols
    slot = jnp.where(col < HALO, left, jnp.where(col >= HALO + shape.cols, right, middle))
    return jnp.clip(slot, 0, shape.slots - 1)


def cell_points(ref, slot, shape):
    block = ref[slot]
    return [block[i * shape.sub : (i + 1) * shape.sub] for i in range(3)]


def put_rows(ref, sub, first, values):
    for i, value in enumerate(values):
        ref[(first + i) * sub : (first + i + 1) * sub, :] = value


def prepare_source(y, f, side_ref, coef_ref, gs_ref, gc_ref, base, shape):
    sub = shape.sub
    square = y[0] * y[0] + y[1] * y[1] + y[2] * y[2]
    split = [pieces(v) for v in (-2.0 * y[0], -2.0 * y[1], -2.0 * y[2], square + soften)]
    for p in range(3):
        rows = [split[0][p], split[1][p], split[2][p]]
        put_rows(gs_ref, sub, 8 * p, rows)
        put_rows(gs_ref, sub, 8 * p + 4, [split[3][p]])
    along = y[0] * f[0] + y[1] * f[1] + y[2] * f[2]
    line = [f[0], f[1], f[2], along]
    values = list(line)
    for i in range(3):
        values += [y[i] * v for v in line]
    values += [square * v for v in f]
    count = len(values)
    for r, value in enumerate(values):
        for p, piece in enumerate(pieces(value)):
            put_rows(gc_ref, sub, p * count + r, [piece])
    for k in range(sub):
        h, m, l = [strided(gs_ref, p * 8 * sub + k, 8, sub) for p in range(3)]
        block = jnp.concatenate([h, m, h, l, h, m], axis=0).T.astype(bf16)
        side_ref[base + k * LANES : base + (k + 1) * LANES, :] = block
        rows = strided(gc_ref, k, coef_ref.shape[0], sub)
        coef_ref[:, base + k * LANES : base + (k + 1) * LANES] = rows.astype(bf16)


def finish(x, total):
    line = x[0] * total(0) + x[1] * total(1) + x[2] * total(2) - total(3)
    square = x[0] * x[0] + x[1] * x[1] + x[2] * x[2] + 2.0 * soften
    low = [total(i) for i in range(3)]
    near = [[total(4 + 4 * j + i) for i in range(4)] for j in range(3)]
    far = [total(16 + i) for i in range(3)]
    out = []
    for i in range(3):
        cross = x[0] * near[0][i] + x[1] * near[1][i] + x[2] * near[2][i]
        turned = x[0] * near[i][0] + x[1] * near[i][1] + x[2] * near[i][2] - near[i][3]
        direct = square * low[i] + far[i] - 2.0 * cross
        out.append(stokes_scale * (direct + x[i] * line - turned))
    return out


COEF = 19


def mega_kernel(
    shape,
    listed,
    near_ref,
    drag_ref,
    pos_ref,
    analysis_hbm,
    stiffness_ref,
    synthesis_hbm,
    wpos_ref,
    wnormal_ref,
    wweight_ref,
    wdensity_ref,
    pnear_ref,
    cpatch_ref,
    moved_ref,
    dens_ref,
    analysis_ref,
    synthesis_ref,
    e_ref,
    f_ref,
    v_ref,
    gs_ref,
    gc_ref,
    gt_ref,
    side_ref,
    coef_ref,
    feat_ref,
    h_ref,
    hp_ref,
    hn_ref,
    hd_ref,
    hw_ref,
    gd_ref,
    gq_ref,
    gm_ref,
    gf_ref,
    gw_ref,
    lside_ref,
    lmom_ref,
    lfeat_ref,
    wfeat_ref,
    lacc_ref,
    wacc_ref,
    mine_ref,
    row_ref,
    from_y,
    from_x,
    local,
    xsend,
    xrecv,
    ysend,
    yrecv,
    wsend,
    wrecv,
    tsend_y,
    trecv_y,
    tsend_x,
    trecv_x,
):
    me_x, me_y = lax.axis_index("cx"), lax.axis_index("cy")
    e_cells, f_cells = e_ref, f_ref
    e_ref = e_cells.reshape(e_cells.shape[0] * e_cells.shape[1], LANES)
    f_ref = f_cells.reshape(f_cells.shape[0] * f_cells.shape[1], LANES)
    size_x, size_y = shape.size_x, shape.size_y
    rows, cols, sub, cell = shape.rows, shape.cols, shape.sub, shape.cell
    patches, wpoints = wpos_ref.shape[1], wpos_ref.shape[2]
    wtiles = wpoints // LANES

    weights = [
        pltpu.make_async_copy(analysis_hbm, analysis_ref, local.at[0]),
        pltpu.make_async_copy(synthesis_hbm, synthesis_ref, local.at[1]),
    ]
    for copy in weights:
        copy.start()

    def around(step_x, step_y):
        return (lax.rem(me_x + step_x + size_x, size_x), lax.rem(me_y + step_y + size_y, size_y))

    def along_walls(step):
        other = lax.rem(me_x * size_y + me_y + step + size_x * size_y, size_x * size_y)
        there = lax.div(other, jnp.int32(size_y))
        return (there, other - there * size_y)

    peers_y = [around(0, d) for d in range(1, size_y)]
    peers_x = [around(d, 0) for d in range(1, size_x)]
    after, before = along_walls(1), along_walls(-1)
    greeted = peers_y + peers_x + [after, before]
    barrier = pltpu.get_barrier_semaphore()
    for device in greeted:
        pl.semaphore_signal(barrier, inc=1, device_id=device, device_id_type=MESH)

    for r in range(rows):
        for c in range(cols):
            for i in range(3):
                at = ((r * cols + c) * 3 + i) * sub
                e_ref[at : at + sub, :] = strided(pos_ref, (r * 3 + i) * sub * cols + c, sub, cols)
    e_ref[shape.slots * cell :, :] = jnp.zeros_like(e_ref[shape.slots * cell :, :])
    for ref in (gs_ref, gc_ref, gt_ref, gd_ref, gq_ref, gm_ref, gf_ref, gw_ref):
        ref[...] = jnp.zeros_like(ref)
    one = jnp.ones((sub, LANES), f32)
    gs_ref[3 * sub : 4 * sub, :] = one
    gt_ref[4 * sub : 5 * sub, :] = one

    pl.semaphore_wait(barrier, len(greeted))

    def remote(src, dst, send, recv, device):
        return pltpu.make_async_remote_copy(
            src_ref=src,
            dst_ref=dst,
            send_sem=send,
            recv_sem=recv,
            device_id=device,
            device_id_type=MESH,
        )

    def cells(slot, count):
        return e_cells.at[slot : slot + count]

    xs = []
    for j in range(HALO):
        k = 2 * j
        up = remote(
            cells((rows - HALO + j) * cols, cols),
            cells((rows + HALO + j) * cols, cols),
            xsend.at[k], xrecv.at[k], around(1, 0),
        )
        down = remote(
            cells(j * cols, cols), cells((rows + j) * cols, cols),
            xsend.at[k + 1], xrecv.at[k + 1], around(-1, 0),
        )
        xs += [(up, rows + HALO + j), (down, rows + j)]

    def sideways(row):
        right = remote(
            cells(row * cols + cols - HALO, HALO), cells(shape.left + row * HALO, HALO),
            ysend.at[2 * row], yrecv.at[2 * row], around(0, 1),
        )
        left = remote(
            cells(row * cols, HALO), cells(shape.right + row * HALO, HALO),
            ysend.at[2 * row + 1], yrecv.at[2 * row + 1], around(0, -1),
        )
        return [right, left]

    ws = []
    sources = ((wpos_ref, hp_ref), (wnormal_ref, hn_ref), (wdensity_ref, hd_ref), (wweight_ref, hw_ref))
    for b, device in enumerate((after, before)):
        for src, dst in sources:
            k = len(ws)
            ws.append(remote(src, dst.at[b], wsend.at[k], wrecv.at[k], device))

    for copy, _ in xs:
        copy.start()
    for copy in ws:
        copy.start()
    ys = []
    for row in range(rows):
        for copy in sideways(row):
            copy.start()
            ys.append(copy)

    x = [wpos_ref[i] for i in range(3)]
    lone = jnp.ones((patches, wpoints), f32)
    squares = [x[i] * x[i] for i in range(3)]
    mono = x + [lone] + squares + [x[0] * x[1], x[0] * x[2], x[1] * x[2]]
    square = squares[0] + squares[1] + squares[2]
    for r, value in enumerate(mono):
        for p, piece in enumerate(pieces(value)):
            put_wide(gf_ref, (16 * p + r) * patches, piece)
    for r, value in enumerate(x + [square, lone]):
        for p, piece in enumerate(pieces(value)):
            put_wide(gw_ref, (8 * p + r) * patches, piece)
    for q in range(patches):
        h, m, l = [get_wide(gf_ref, wtiles, p * 16 * patches + q, 16, patches) for p in range(3)]
        lfeat_ref[q * 96 : (q + 1) * 96, :] = jnp.concatenate([h, h, m, h, l, m], axis=0).astype(bf16)
        h, m, l = [get_wide(gw_ref, wtiles, p * 8 * patches + q, 8, patches) for p in range(3)]
        wfeat_ref[q * 48 : (q + 1) * 48, :] = jnp.concatenate([h, h, m, h, l, m], axis=0).astype(bf16)

    def wall_sources(b, y, n, v, w):
        w = -layer_scale * w
        v = [w * value for value in v]
        zero = jnp.zeros_like(w)
        ones = jnp.ones_like(w)
        square = y[0] * y[0] + y[1] * y[1] + y[2] * y[2] + soften
        dist = [-2.0 * y[0], -2.0 * y[1], -2.0 * y[2], square, ones, ones, ones]
        a = y[0] * v[0] + y[1] * v[1] + y[2] * v[2]
        c = y[0] * n[0] + y[1] * n[1] + y[2] * n[2]
        quad = [-(v[i] * c + n[i] * a) for i in range(3)] + [a * c]
        quad += [v[i] * n[i] for i in range(3)]
        quad += [v[i] * n[j] + v[j] * n[i] for i, j in ((0, 1), (0, 2), (1, 2))]
        for values, ref in ((dist, gd_ref), (quad, gq_ref)):
            for r, value in enumerate(values):
                for p, piece in enumerate(pieces(value)):
                    put_wide(ref, (16 * p + r) * patches, piece)
        for r, value in enumerate(y + [ones]):
            for p, piece in enumerate(pieces(value)):
                if p == 0 or r < 3:
                    put_wide(gm_ref, (4 * p + r) * patches, piece)

        def one_patch(q, _):
            slot = b * patches + q
            for s, ref in enumerate((gd_ref, gq_ref)):
                for k in range(wtiles):
                    h, m, l = [
                        get_tile(ref, wtiles, k, p * 16 * patches + q, 16, patches) for p in range(3)
                    ]
                    block = jnp.concatenate([h, m, h, l, h, m], axis=0).T.astype(bf16)
                    at = s * wpoints + k * LANES
                    lside_ref[slot, at : at + LANES, :] = block
            rows16 = get_wide(gm_ref, wtiles, q, 16, patches)
            lmom_ref[slot] = rows16.astype(bf16)
            return 0

        lax.fori_loop(0, patches, one_patch, 0)

    wall_sources(
        1, x, [wnormal_ref[i] for i in range(3)], [wdensity_ref[i] for i in range(3)], wweight_ref[...]
    )

    for copy in weights:
        copy.wait()

    def membrane(first, count):
        tiles = [strided(e_ref, first * sub + k, count, sub) for k in range(sub)]
        value = jnp.concatenate(tiles, axis=1)
        centred = (value - jnp.mean(value, axis=1, keepdims=True)).astype(bf16)
        coeff = jnp.dot(centred, analysis_ref[...], preferred_element_type=f32)
        scaled = (coeff * stiffness_ref[...]).astype(bf16)
        force = -jnp.dot(scaled, synthesis_ref[...], preferred_element_type=f32)
        for k in range(sub):
            f_ref[pl.ds(first * sub + k, count, stride=sub), :] = force[:, k * LANES : (k + 1) * LANES]

    membrane(0, 3 * rows * cols)

    for copy in ws:
        copy.wait_recv()
    for b in range(2):
        wall_sources(
            2 * b,
            [hp_ref[b, i] for i in range(3)],
            [hn_ref[b, i] for i in range(3)],
            [hd_ref[b, i] for i in range(3)],
            hw_ref[b],
        )

    for copy, row in xs:
        copy.wait_recv()
        for onward in sideways(row):
            onward.start()
            ys.append(onward)

    all_patches = patches * size_x * size_y
    block_start = (me_x * size_y + me_y) * patches

    def put_patch(ref, t, value):
        height = ref.shape[0] // wtiles
        for k in range(wtiles):
            at = pl.multiple_of(k * height + t * value.shape[0], 8)
            ref[pl.ds(at, value.shape[0]), :] = value[:, k * LANES : (k + 1) * LANES]

    def layer_patch(t, _):
        feat = lfeat_ref[pl.ds(pl.multiple_of(t * 96, 16), 96), :]
        total = None
        for n in range(listed + 1):
            if n == 0:
                slot = t + patches
            else:
                slot = pnear_ref[n - 1, t] - block_start + patches
                slot = jnp.where(slot < 0, slot + all_patches, slot)
                slot = jnp.where(slot >= all_patches, slot - all_patches, slot)
                slot = jnp.clip(slot, 0, 3 * patches - 1)
            side = lside_ref[slot]
            both = jnp.dot(side, feat, preferred_element_type=f32)
            root = lax.rsqrt(both[:wpoints])
            square = root * root
            scalar = (both[wpoints:] * (square * square * root)).astype(bf16)
            moment = lmom_ref[slot]
            part = jnp.dot(moment, scalar, preferred_element_type=f32)
            total = part if total is None else total + part
        put_patch(lacc_ref, t, total)
        return 0

    lax.fori_loop(0, patches, layer_patch, 0)

    membrane(3 * rows * cols, 3 * 2 * HALO * cols)
    for copy in ys:
        copy.wait_recv()
    membrane(3 * shape.left, -(-3 * (shape.slots - shape.left) // 8) * 8)

    def cell_step(i, best):
        r = lax.div(i, jnp.int32(cols))
        c = i - r * cols
        x = cell_points(e_cells, i, shape)
        square = x[0] * x[0] + x[1] * x[1] + x[2] * x[2]
        split = [pieces(v) for v in (x[0], x[1], x[2], square)]
        for p in range(3):
            put_rows(gt_ref, sub, 8 * p, [s[p] for s in split])
        for k in range(sub):
            h, m, l = [strided(gt_ref, p * 8 * sub + k, 8, sub) for p in range(3)]
            feat_ref[:, k * LANES : (k + 1) * LANES] = jnp.concatenate(
                [h, h, m, h, l, m], axis=0
            ).astype(bf16)
        for n in range(shape.near):
            slot = cell_slot(shape, near_ref[r, n, c], me_x, me_y)
            prepare_source(
                cell_points(e_cells, slot, shape), cell_points(f_cells, slot, shape),
                side_ref, coef_ref, gs_ref, gc_ref, n * shape.points, shape,
            )
        side = side_ref[...]
        coef = coef_ref[...]
        for t in range(shape.points // WIDTH):
            root = lax.rsqrt(
                jnp.dot(side, feat_ref[:, t * WIDTH : (t + 1) * WIDTH], preferred_element_type=f32)
            )
            cube = (root * root * root).astype(bf16)
            acc = jnp.dot(coef, cube, preferred_element_type=f32)
            for k in range(WIDTH // LANES):
                tile = t * (WIDTH // LANES) + k
                h_ref[pl.ds(tile, acc.shape[0], stride=sub), :] = acc[:, k * LANES : (k + 1) * LANES]

        def total(row):
            a, b, d = [h_ref[(p * COEF + row) * sub : (p * COEF + row + 1) * sub, :] for p in range(3)]
            return a + (b + d)

        parts = finish(x, total)
        own = cell_points(f_cells, i, shape)
        drag = drag_ref[r, c]
        squared = jnp.zeros_like(best)
        values = []
        for k in range(3):
            value = drag * own[k] + parts[k]
            values.append(value)
            squared = squared + value * value
        v_ref[pl.ds(pl.multiple_of(i * cell, 8), cell), :] = jnp.concatenate(values, axis=0)
        return jnp.maximum(best, squared)

    best = lax.fori_loop(0, rows * cols, cell_step, jnp.zeros((sub, LANES), f32))
    mine_ref[...] = best

    def wall_step(t, _):
        for n in range(cpatch_ref.shape[0]):
            slot = cell_slot(shape, cpatch_ref[n, t], me_x, me_y)
            prepare_source(
                cell_points(e_cells, slot, shape), cell_points(f_cells, slot, shape),
                side_ref, coef_ref, gs_ref, gc_ref, n * shape.points, shape,
            )
        feat = wfeat_ref[pl.ds(pl.multiple_of(t * 48, 16), 48), :]
        acc = None
        for n in range(cpatch_ref.shape[0]):
            part = slice(n * shape.points, (n + 1) * shape.points)
            root = lax.rsqrt(jnp.dot(side_ref[part, :], feat, preferred_element_type=f32))
            cube = (root * root * root).astype(bf16)
            more = jnp.dot(coef_ref[:, part], cube, preferred_element_type=f32)
            acc = more if acc is None else acc + more
        put_patch(wacc_ref, t, acc)
        return 0

    lax.fori_loop(0, 1, wall_step, 0)
    copies = []
    for d, device in enumerate(peers_y):
        copies.append(remote(mine_ref, from_y.at[d], tsend_y.at[d], trecv_y.at[d], device))
        copies[-1].start()
    lax.fori_loop(1, patches // 2, wall_step, 0)
    best = mine_ref[...]
    for d, copy in enumerate(copies):
        copy.wait_recv()
        best = jnp.maximum(best, from_y[d])
    row_ref[...] = best
    lax.fori_loop(patches // 2, patches // 2 + 1, wall_step, 0)
    for d, device in enumerate(peers_x):
        copies.append(remote(row_ref, from_x.at[d], tsend_x.at[d], trecv_x.at[d], device))
        copies[-1].start()
    lax.fori_loop(patches // 2 + 1, patches, wall_step, 0)

    def wall_total(row):
        a, b, d = [
            get_wide(wacc_ref, wtiles, p * COEF + row, patches, coef_ref.shape[0]) for p in range(3)
        ]
        return a + (b + d)

    flow = finish(x, wall_total)
    moment = [get_wide(lacc_ref, wtiles, r, patches, 16) for r in range(11)]
    moment = [moment[i] + (moment[4 + i] + moment[8 + i]) for i in range(3)] + [moment[3]]
    for i in range(3):
        layer = x[i] * moment[3] - moment[i]
        dens_ref[i] = 2.0 * layer + 2.0 * flow[i]

    best = row_ref[...]
    for d, copy in enumerate(copies[size_y - 1 :]):
        copy.wait_recv()
        best = jnp.maximum(best, from_x[d])
    top = jnp.sqrt(jnp.max(best, keepdims=True))
    step = 1.0 / (top + 1e-06)
    for r in range(rows):
        for c in range(cols):
            for i in range(3):
                at = ((r * cols + c) * 3 + i) * sub
                value = e_ref[at : at + sub, :] + step * v_ref[at : at + sub, :]
                moved_ref[pl.ds((r * 3 + i) * sub * cols + c, sub, stride=cols), :] = value
    for copy, _ in xs:
        copy.wait_send()
    for copy in ws + ys + copies:
        copy.wait_send()


def body(
    cell_pos,
    cell_drag,
    cell_near,
    analysis,
    stiffness,
    synthesis,
    wall_pos,
    wall_normal,
    wall_weight,
    density,
    patch_near,
    cell_to_patch,
):
    rows, cols, _, points = cell_pos.shape
    size_x, size_y = lax.axis_size("cx"), lax.axis_size("cy")
    near = cell_near.shape[2]
    listed = patch_near.shape[1]
    patches, _, wpoints = wall_pos.shape
    shape = Shape(rows, cols, points, size_x, size_y, near)
    sub, cell = shape.sub, shape.cell
    raw = cell_pos.reshape(rows, cols, 3, sub, LANES)
    raw = jnp.transpose(raw, (0, 2, 3, 1, 4)).reshape(rows * 3 * sub * cols, LANES)
    wtiles = wpoints // LANES
    spare = -(-shape.slots // 8) * 8
    sources = near * points
    assert cell_to_patch.shape[1] == near
    coef_rows = -(-3 * COEF // 16) * 16
    dma = pltpu.SemaphoreType.DMA
    vmem = pltpu.VMEM
    in_vmem = pl.BlockSpec(memory_space=pltpu.VMEM)
    in_smem = pl.BlockSpec(memory_space=pltpu.SMEM)
    in_hbm = pl.BlockSpec(memory_space=pl.ANY)
    walls = lambda v: jnp.transpose(v, (1, 0, 2))
    moved, dens = pl.pallas_call(
        functools.partial(mega_kernel, shape, listed),
        out_shape=(
            jax.ShapeDtypeStruct(raw.shape, f32),
            jax.ShapeDtypeStruct((3, patches, wpoints), f32),
        ),
        in_specs=[
            in_smem, in_smem, in_vmem, in_hbm, in_vmem, in_hbm,
            in_vmem, in_vmem, in_vmem, in_vmem, in_smem, in_smem,
        ],
        out_specs=[in_vmem, in_vmem],
        scratch_shapes=[
            vmem(analysis.shape, bf16),
            vmem(synthesis.shape, bf16),
            vmem((spare, cell, LANES), f32),
            vmem((spare, cell, LANES), f32),
            vmem((rows * cols * cell, LANES), f32),
            vmem((24 * sub, LANES), f32),
            vmem((coef_rows * sub, LANES), f32),
            vmem((24 * sub, LANES), f32),
            vmem((sources, 48), bf16),
            vmem((coef_rows, sources), bf16),
            vmem((48, points), bf16),
            vmem((coef_rows * sub, LANES), f32),
            vmem((2, 3, patches, wpoints), f32),
            vmem((2, 3, patches, wpoints), f32),
            vmem((2, 3, patches, wpoints), f32),
            vmem((2, patches, wpoints), f32),
            vmem((48 * patches * wtiles, LANES), f32),
            vmem((48 * patches * wtiles, LANES), f32),
            vmem((16 * patches * wtiles, LANES), f32),
            vmem((48 * patches * wtiles, LANES), f32),
            vmem((24 * patches * wtiles, LANES), f32),
            vmem((3 * patches, 2 * wpoints, 96), bf16),
            vmem((3 * patches, 16, wpoints), bf16),
            vmem((patches * 96, wpoints), bf16),
            vmem((patches * 48, wpoints), bf16),
            vmem((patches * 16 * wtiles, LANES), f32),
            vmem((patches * coef_rows * wtiles, LANES), f32),
            vmem((sub, LANES), f32),
            vmem((sub, LANES), f32),
            vmem((size_y - 1, sub, LANES), f32),
            vmem((size_x - 1, sub, LANES), f32),
            dma((2,)),
            dma((2 * HALO,)),
            dma((2 * HALO,)),
            dma((2 * shape.ext_rows,)),
            dma((2 * shape.ext_rows,)),
            dma((8,)),
            dma((8,)),
            dma((size_y - 1,)),
            dma((size_y - 1,)),
            dma((size_x - 1,)),
            dma((size_x - 1,)),
        ],
        compiler_params=pltpu.CompilerParams(
            collective_id=0, has_side_effects=True, vmem_limit_bytes=56 * 2**20
        ),
        name="mega",
    )(
        jnp.transpose(cell_near, (0, 2, 1)),
        cell_drag,
        raw,
        analysis,
        stiffness[None, :],
        synthesis,
        walls(wall_pos),
        walls(wall_normal),
        wall_weight,
        walls(density),
        jnp.transpose(patch_near),
        jnp.transpose(cell_to_patch),
    )
    moved = jnp.transpose(moved.reshape(rows, 3, sub, cols, LANES), (0, 3, 1, 2, 4))
    return moved.reshape(cell_pos.shape), jnp.transpose(dens, (1, 0, 2))


def solution(mesh):
    placed = (
        P("cx", "cy", None, None),
        P("cx", "cy"),
        P("cx", "cy", None),
        P(),
        P(),
        P(),
        P(("cx", "cy"), None, None),
        P(("cx", "cy"), None, None),
        P(("cx", "cy"), None),
        P(("cx", "cy"), None, None),
        P(("cx", "cy"), None),
        P(("cx", "cy"), None),
    )
    return jax.shard_map(
        body,
        mesh=mesh,
        in_specs=placed,
        out_specs=(P("cx", "cy", None, None), P(("cx", "cy"), None, None)),
        check_vma=False,
    )
```

time: 120 us -> 78.4 us (0.65)
  Pallas kernels: 104 us -> 74.5 us
  local copies, waits for them, and re-layouts: 8.81 us -> 2.96 us
  other arithmetic: 5.1 us -> 0 us
    pallas_call x5 -> x1, Pallas kernels: 104 us -> 74.5 us  [body(): pl.pallas_call(functools.partial(mega_kernel, shape, listed), out_shape=(...]
    unnamed x13 -> x2, local copies, waits for them, and re-layouts: 6.16 us -> 2.96 us
    add x5 -> x0, other arithmetic: 2.72 us -> none  [the longest x2 1.34 us: local_slot(): return local_row * ext_cols + local_col]
    reshape x2 -> x0, local copies, waits for them, and re-layouts: 1.95 us -> none  [the longest x1 1.24 us: body(): cell_drag.reshape(count)]
    concatenate x2 -> x0, other arithmetic: 1.37 us -> none  [the longest x1 0.7 us: body(): jnp.concatenate([wall_pos, wall_normal, density, wall_weight[:, None, :]]...]
where the time goes in v1:
time: 78.4 us; the launch traced here: 78.1 us
  Pallas kernels  74.5 us (95%)
  local copies, waits for them, and re-layouts  2.96 us (4%)
    pallas_call x1, Pallas kernels, body(): pl.pallas_call(functools.partial(mega_kernel, shape, listed), out_shape=(...  74.5 us
    unnamed x2, local copies, waits for them, and re-layouts  2.96 us

profile of v1, /device:TPU:0, one launch (start us, length us, event | category | flops | bytes accessed | tf_op | source)
XLA Modules:
  0.0 78.1 jit_solution(13070812146192368989)
XLA Ops:
  0.6 74.5 %mega.1 = (f32[384,128]{1,0:T(8,128)}, f32[3,8,256]{2,1,0:T(8,128)}) custom-call(s32[4,2,4]{2,1,0:T(2,128)} %bitcast.24, f32[4,4]{1,0:T(4,128)} %drag_ref.1, f32[384,128]{1,0:T(8,128)} %bitcast.18, bf16[1024,1024]{1,0:T(8,128)(2,1)} %analysis_hbm.1, f32[1,1024]{1,0:T(1,128)} %bitcast.25, bf16[1024,1024]{1,0:T(8,128)(2,1)} %synthesis_hbm.1, ...), custom_call_target="tpu_custom_call" | custom-call | tf_op jit(solution)/shard_map/mega/pallas_call | solution.py:574
  75.2 1.6 %copy.18 = f32[4,4,3,1024]{3,1,2,0:T(4,128)} copy(f32[4,4,3,1024]{3,1,2,0:T(4,128)} %bitcast.19) | data formatting | bytes 393216
  76.8 1.3 %copy.19 = f32[8,3,256]{2,0,1:T(8,128)} copy(f32[8,3,256]{2,0,1:T(8,128)} %bitcast.23) | data formatting | bytes 49152

commit v2 on v1

--- a/solution.py
+++ b/solution.py
@@ -147,19 +147,24 @@
     wdensity_ref,
     pnear_ref,
     cpatch_ref,
-    moved_ref,
-    dens_ref,
+    speed_ref,
+    top_ref,
+    half_ref,
     analysis_ref,
     synthesis_ref,
     e_ref,
     f_ref,
     v_ref,
-    gs_ref,
-    gc_ref,
+    gs_a,
+    gs_b,
+    gc_a,
+    gc_b,
     gt_ref,
     side_ref,
     coef_ref,
-    feat_ref,
+    feats_ref,
+    cube_a,
+    cube_b,
     h_ref,
     hp_ref,
     hn_ref,
@@ -196,6 +201,7 @@
     e_cells, f_cells = e_ref, f_ref
     e_ref = e_cells.reshape(e_cells.shape[0] * e_cells.shape[1], LANES)
     f_ref = f_cells.reshape(f_cells.shape[0] * f_cells.shape[1], LANES)
+    gs, gc, cubes = (gs_a, gs_b), (gc_a, gc_b), (cube_a, cube_b)
     size_x, size_y = shape.size_x, shape.size_y
     rows, cols, sub, cell = shape.rows, shape.cols, shape.sub, shape.cell
     patches, wpoints = wpos_ref.shape[1], wpos_ref.shape[2]
@@ -230,10 +236,11 @@
                 at = ((r * cols + c) * 3 + i) * sub
                 e_ref[at : at + sub, :] = strided(pos_ref, (r * 3 + i) * sub * cols + c, sub, cols)
     e_ref[shape.slots * cell :, :] = jnp.zeros_like(e_ref[shape.slots * cell :, :])
-    for ref in (gs_ref, gc_ref, gt_ref, gd_ref, gq_ref, gm_ref, gf_ref, gw_ref):
+    for ref in (*gs, *gc, gt_ref, gd_ref, gq_ref, gm_ref, gf_ref, gw_ref):
         ref[...] = jnp.zeros_like(ref)
     one = jnp.ones((sub, LANES), f32)
-    gs_ref[3 * sub : 4 * sub, :] = one
+    for ref in gs:
+        ref[3 * sub : 4 * sub, :] = one
     gt_ref[4 * sub : 5 * sub, :] = one
 
     pl.semaphore_wait(barrier, len(greeted))
@@ -292,6 +299,21 @@
         for copy in sideways(row):
             copy.start()
             ys.append(copy)
+
+    def target(i, _):
+        x = cell_points(e_cells, i, shape)
+        square = x[0] * x[0] + x[1] * x[1] + x[2] * x[2]
+        split = [pieces(v) for v in (x[0], x[1], x[2], square)]
+        for p in range(3):
+            put_rows(gt_ref, sub, 8 * p, [s[p] for s in split])
+        tiles = []
+        for k in range(sub):
+            h, m, l = [strided(gt_ref, p * 8 * sub + k, 8, sub) for p in range(3)]
+            tiles.append(jnp.concatenate([h, h, m, h, l, m], axis=0).astype(bf16))
+        feats_ref[i] = jnp.concatenate(tiles, axis=1)
+        return 0
+
+    lax.fori_loop(0, rows * cols, target, 0)
 
     x = [wpos_ref[i] for i in range(3)]
     lone = jnp.ones((patches, wpoints), f32)
@@ -377,11 +399,12 @@
             hw_ref[b],
         )
 
-    for copy, row in xs:
-        copy.wait_recv()
-        for onward in sideways(row):
-            onward.start()
-            ys.append(onward)
+    def pass_on(pairs):
+        for copy, row in pairs:
+            copy.wait_recv()
+            for onward in sideways(row):
+                onward.start()
+                ys.append(onward)
 
     all_patches = patches * size_x * size_y
     block_start = (me_x * size_y + me_y) * patches
@@ -414,43 +437,63 @@
         put_patch(lacc_ref, t, total)
         return 0
 
-    lax.fori_loop(0, patches, layer_patch, 0)
+    done = 0
+    for j in range(HALO):
+        pass_on(xs[2 * j : 2 * j + 2])
+        upto = patches if j == HALO - 1 else (j + 1) * patches // 4
+        lax.fori_loop(done, upto, layer_patch, 0)
+        done = upto
 
     membrane(3 * rows * cols, 3 * 2 * HALO * cols)
     for copy in ys:
         copy.wait_recv()
     membrane(3 * shape.left, -(-3 * (shape.slots - shape.left) // 8) * 8)
 
-    def cell_step(i, best):
+    def cell_prepare(i):
         r = lax.div(i, jnp.int32(cols))
         c = i - r * cols
-        x = cell_points(e_cells, i, shape)
-        square = x[0] * x[0] + x[1] * x[1] + x[2] * x[2]
-        split = [pieces(v) for v in (x[0], x[1], x[2], square)]
-        for p in range(3):
-            put_rows(gt_ref, sub, 8 * p, [s[p] for s in split])
-        for k in range(sub):
-            h, m, l = [strided(gt_ref, p * 8 * sub + k, 8, sub) for p in range(3)]
-            feat_ref[:, k * LANES : (k + 1) * LANES] = jnp.concatenate(
-                [h, h, m, h, l, m], axis=0
-            ).astype(bf16)
         for n in range(shape.near):
             slot = cell_slot(shape, near_ref[r, n, c], me_x, me_y)
             prepare_source(
                 cell_points(e_cells, slot, shape), cell_points(f_cells, slot, shape),
-                side_ref, coef_ref, gs_ref, gc_ref, n * shape.points, shape,
+                side_ref, coef_ref, gs[n], gc[n], n * shape.points, shape,
             )
-        side = side_ref[...]
-        coef = coef_ref[...]
-        for t in range(shape.points // WIDTH):
-            root = lax.rsqrt(
-                jnp.dot(side, feat_ref[:, t * WIDTH : (t + 1) * WIDTH], preferred_element_type=f32)
-            )
-            cube = (root * root * root).astype(bf16)
-            acc = jnp.dot(coef, cube, preferred_element_type=f32)
-            for k in range(WIDTH // LANES):
-                tile = t * (WIDTH // LANES) + k
-                h_ref[pl.ds(tile, acc.shape[0], stride=sub), :] = acc[:, k * LANES : (k + 1) * LANES]
+
+    chunks = shape.points // WIDTH
+    sources = shape.near * shape.points
+    steps = [slice(at, at + WIDTH) for at in range(0, sources, WIDTH)]
+
+    def weigh(part, cube_ref):
+        return jnp.dot(coef_ref[:, part], cube_ref[part, :], preferred_element_type=f32)
+
+    def keep(t, acc):
+        for k in range(WIDTH // LANES):
+            tile = t * (WIDTH // LANES) + k
+            h_ref[pl.ds(tile, acc.shape[0], stride=sub), :] = acc[:, k * LANES : (k + 1) * LANES]
+
+    def cell_sums(i):
+        last = None
+        for t in range(chunks):
+            feat = feats_ref[i, :, t * WIDTH : (t + 1) * WIDTH]
+            acc = None
+            for part in steps:
+                root = lax.rsqrt(jnp.dot(side_ref[part, :], feat, preferred_element_type=f32))
+                cubes[t % 2][part, :] = (root * root * root).astype(bf16)
+                if t > 0:
+                    more = weigh(part, cubes[(t - 1) % 2])
+                    acc = more if acc is None else acc + more
+            if t > 0:
+                keep(t - 1, acc)
+        acc = None
+        for part in steps:
+            more = weigh(part, cubes[(chunks - 1) % 2])
+            acc = more if acc is None else acc + more
+        keep(chunks - 1, acc)
+
+    def cell_finish(i, best):
+        r = lax.div(i, jnp.int32(cols))
+        c = i - r * cols
+        x = cell_points(e_cells, i, shape)
 
         def total(row):
             a, b, d = [h_ref[(p * COEF + row) * sub : (p * COEF + row + 1) * sub, :] for p in range(3)]
@@ -468,16 +511,24 @@
         v_ref[pl.ds(pl.multiple_of(i * cell, 8), cell), :] = jnp.concatenate(values, axis=0)
         return jnp.maximum(best, squared)
 
+    def cell_step(i, best):
+        cell_sums(i)
+        cell_prepare(jnp.minimum(i + 1, rows * cols - 1))
+        return cell_finish(i, best)
+
+    cell_prepare(jnp.int32(0))
     best = lax.fori_loop(0, rows * cols, cell_step, jnp.zeros((sub, LANES), f32))
     mine_ref[...] = best
 
-    def wall_step(t, _):
+    def wall_prepare(t):
         for n in range(cpatch_ref.shape[0]):
             slot = cell_slot(shape, cpatch_ref[n, t], me_x, me_y)
             prepare_source(
                 cell_points(e_cells, slot, shape), cell_points(f_cells, slot, shape),
-                side_ref, coef_ref, gs_ref, gc_ref, n * shape.points, shape,
+                side_ref, coef_ref, gs[n], gc[n], n * shape.points, shape,
             )
+
+    def wall_step(t, _):
         feat = wfeat_ref[pl.ds(pl.multiple_of(t * 48, 16), 48), :]
         acc = None
         for n in range(cpatch_ref.shape[0]):
@@ -487,24 +538,26 @@
             more = jnp.dot(coef_ref[:, part], cube, preferred_element_type=f32)
             acc = more if acc is None else acc + more
         put_patch(wacc_ref, t, acc)
+        wall_prepare(jnp.minimum(t + 1, patches - 1))
         return 0
 
-    lax.fori_loop(0, 1, wall_step, 0)
+    wall_prepare(jnp.int32(0))
     copies = []
     for d, device in enumerate(peers_y):
         copies.append(remote(mine_ref, from_y.at[d], tsend_y.at[d], trecv_y.at[d], device))
         copies[-1].start()
-    lax.fori_loop(1, patches // 2, wall_step, 0)
+    half = patches // 2 - 1
+    lax.fori_loop(0, half, wall_step, 0)
     best = mine_ref[...]
     for d, copy in enumerate(copies):
         copy.wait_recv()
         best = jnp.maximum(best, from_y[d])
     row_ref[...] = best
-    lax.fori_loop(patches // 2, patches // 2 + 1, wall_step, 0)
+    lax.fori_loop(half, half + 1, wall_step, 0)
     for d, device in enumerate(peers_x):
         copies.append(remote(row_ref, from_x.at[d], tsend_x.at[d], trecv_x.at[d], device))
         copies[-1].start()
-    lax.fori_loop(patches // 2 + 1, patches, wall_step, 0)
+    lax.fori_loop(half + 1, patches, wall_step, 0)
 
     def wall_total(row):
         a, b, d = [
@@ -517,24 +570,29 @@
     moment = [moment[i] + (moment[4 + i] + moment[8 + i]) for i in range(3)] + [moment[3]]
     for i in range(3):
         layer = x[i] * moment[3] - moment[i]
-        dens_ref[i] = 2.0 * layer + 2.0 * flow[i]
+        half_ref[i] = layer + flow[i]
 
     best = row_ref[...]
     for d, copy in enumerate(copies[size_y - 1 :]):
         copy.wait_recv()
         best = jnp.maximum(best, from_x[d])
-    top = jnp.sqrt(jnp.max(best, keepdims=True))
-    step = 1.0 / (top + 1e-06)
+    top_ref[...] = best
     for r in range(rows):
         for c in range(cols):
             for i in range(3):
                 at = ((r * cols + c) * 3 + i) * sub
-                value = e_ref[at : at + sub, :] + step * v_ref[at : at + sub, :]
-                moved_ref[pl.ds((r * 3 + i) * sub * cols + c, sub, stride=cols), :] = value
+                speed_ref[pl.ds((r * 3 + i) * sub * cols + c, sub, stride=cols), :] = v_ref[at : at + sub, :]
     for copy, _ in xs:
         copy.wait_send()
     for copy in ws + ys + copies:
         copy.wait_send()
+
+
+def update_kernel(pos_ref, speed_ref, top_ref, half_ref, moved_ref, dens_ref):
+    top = jnp.sqrt(jnp.max(top_ref[...], keepdims=True))
+    step = 1.0 / (top + 1e-06)
+    moved_ref[...] = pos_ref[...] + step * speed_ref[...]
+    dens_ref[...] = 2.0 * half_ref[...]
 
 
 def body(
@@ -571,17 +629,18 @@
     in_smem = pl.BlockSpec(memory_space=pltpu.SMEM)
     in_hbm = pl.BlockSpec(memory_space=pl.ANY)
     walls = lambda v: jnp.transpose(v, (1, 0, 2))
-    moved, dens = pl.pallas_call(
+    speed, top, half = pl.pallas_call(
         functools.partial(mega_kernel, shape, listed),
         out_shape=(
             jax.ShapeDtypeStruct(raw.shape, f32),
+            jax.ShapeDtypeStruct((sub, LANES), f32),
             jax.ShapeDtypeStruct((3, patches, wpoints), f32),
         ),
         in_specs=[
             in_smem, in_smem, in_vmem, in_hbm, in_vmem, in_hbm,
             in_vmem, in_vmem, in_vmem, in_vmem, in_smem, in_smem,
         ],
-        out_specs=[in_vmem, in_vmem],
+        out_specs=[in_vmem] * 3,
         scratch_shapes=[
             vmem(analysis.shape, bf16),
             vmem(synthesis.shape, bf16),
@@ -589,11 +648,15 @@
             vmem((spare, cell, LANES), f32),
             vmem((rows * cols * cell, LANES), f32),
             vmem((24 * sub, LANES), f32),
+            vmem((24 * sub, LANES), f32),
+            vmem((coef_rows * sub, LANES), f32),
             vmem((coef_rows * sub, LANES), f32),
             vmem((24 * sub, LANES), f32),
             vmem((sources, 48), bf16),
             vmem((coef_rows, sources), bf16),
-            vmem((48, points), bf16),
+            vmem((rows * cols, 48, points), bf16),
+            vmem((sources, WIDTH), bf16),
+            vmem((sources, WIDTH), bf16),
             vmem((coef_rows * sub, LANES), f32),
             vmem((2, 3, patches, wpoints), f32),
             vmem((2, 3, patches, wpoints), f32),
@@ -627,7 +690,7 @@
             dma((size_x - 1,)),
         ],
         compiler_params=pltpu.CompilerParams(
-            collective_id=0, has_side_effects=True, vmem_limit_bytes=56 * 2**20
+            collective_id=0, has_side_effects=True, vmem_limit_bytes=62 * 2**20
         ),
         name="mega",
     )(
@@ -644,6 +707,16 @@
         jnp.transpose(patch_near),
         jnp.transpose(cell_to_patch),
     )
+    moved, dens = pl.pallas_call(
+        update_kernel,
+        out_shape=(
+            jax.ShapeDtypeStruct(raw.shape, f32),
+            jax.ShapeDtypeStruct((3, patches, wpoints), f32),
+        ),
+        in_specs=[in_vmem] * 4,
+        out_specs=[in_vmem] * 2,
+        name="update",
+    )(raw, speed, top, half)
     moved = jnp.transpose(moved.reshape(rows, 3, sub, cols, LANES), (0, 3, 1, 2, 4))
     return moved.reshape(cell_pos.shape), jnp.transpose(dens, (1, 0, 2))
 

time: 78.4 us -> 71.5 us (0.912)
  Pallas kernels: 74.5 us -> 70.7 us
  local copies, waits for them, and re-layouts: 2.96 us -> 0 us
    pallas_call x1, Pallas kernels: 74.5 us -> 68.8 us  [body(): pl.pallas_call(functools.partial(mega_kernel, shape, listed), out_shape=(...]
    unnamed x2 -> x0, local copies, waits for them, and re-layouts: 2.96 us -> none
    pallas_call x0 -> x1, Pallas kernels: none -> 1.86 us  [body(): pl.pallas_call(update_kernel, out_shape=(jax.ShapeDtypeStruct(raw.shape,...]
where the time goes in v2:
time: 71.5 us; the launch traced here: 71.3 us
  Pallas kernels  70.7 us (99%)
    pallas_call x1, Pallas kernels, body(): pl.pallas_call(functools.partial(mega_kernel, shape, listed), out_shape=(...  68.8 us
    pallas_call x1, Pallas kernels, body(): pl.pallas_call(update_kernel, out_shape=(jax.ShapeDtypeStruct(raw.shape,...  1.86 us

profile of v2, /device:TPU:0, one launch (start us, length us, event | category | flops | bytes accessed | tf_op | source)
XLA Modules:
  0.0 71.3 jit_solution(8161510883266068186)
XLA Ops:
  0.6 68.8 %mega.1 = (f32[384,128]{1,0:T(8,128)}, f32[8,128]{1,0:T(8,128)}, f32[3,8,256]{2,1,0:T(8,128)}) custom-call(s32[4,2,4]{2,1,0:T(2,128)} %bitcast.23, f32[4,4]{1,0:T(4,128)} %drag_ref.1, f32[384,128]{1,0:T(8,128)} %bitcast.18, bf16[1024,1024]{1,0:T(8,128)(2,1)} %analysis_hbm.1, f32[1,1024]{1,0:T(1,128)} %bitcast.24, bf16[1024,1024]{1,0:T(8,128)(2,1)} %synthesis_hbm.1, ...), custom_call_target="tpu_custom_call" | custom-call | tf_op jit(solution)/shard_map/mega/pallas_call | solution.py:632
  69.4 1.9 %update.1 = (f32[384,128]{1,0:T(8,128)}, f32[3,8,256]{2,1,0:T(8,128)}) custom-call(f32[384,128]{1,0:T(8,128)} %bitcast.19, f32[384,128]{1,0:T(8,128)} %get-tuple-element.7.speed_ref, f32[8,128]{1,0:T(8,128)} %get-tuple-element.8.top_ref, f32[3,8,256]{2,1,0:T(8,128)} %get-tuple-element.9.half_ref), custom_call_target="tpu_custom_call" | custom-call | tf_op jit(solution)/shard_map/update/pallas_call | solution.py:710

commit v3 on v2

--- a/solution.py
+++ b/solution.py
@@ -88,30 +88,36 @@
         ref[(first + i) * sub : (first + i + 1) * sub, :] = value
 
 
-def prepare_source(y, f, side_ref, coef_ref, gs_ref, gc_ref, base, shape):
-    sub = shape.sub
-    square = y[0] * y[0] + y[1] * y[1] + y[2] * y[2]
-    split = [pieces(v) for v in (-2.0 * y[0], -2.0 * y[1], -2.0 * y[2], square + soften)]
-    for p in range(3):
-        rows = [split[0][p], split[1][p], split[2][p]]
-        put_rows(gs_ref, sub, 8 * p, rows)
-        put_rows(gs_ref, sub, 8 * p + 4, [split[3][p]])
-    along = y[0] * f[0] + y[1] * f[1] + y[2] * f[2]
-    line = [f[0], f[1], f[2], along]
-    values = list(line)
-    for i in range(3):
-        values += [y[i] * v for v in line]
-    values += [square * v for v in f]
-    count = len(values)
-    for r, value in enumerate(values):
-        for p, piece in enumerate(pieces(value)):
-            put_rows(gc_ref, sub, p * count + r, [piece])
+def prepare_sources(sources, side_ref, coef_ref, gs, gc, shape):
+    sub, points = shape.sub, shape.points
+    for n, (y, f) in enumerate(sources):
+        square = y[0] * y[0] + y[1] * y[1] + y[2] * y[2]
+        split = [pieces(v) for v in (-2.0 * y[0], -2.0 * y[1], -2.0 * y[2], square + soften)]
+        for p in range(3):
+            put_rows(gs[n], sub, 8 * p, [split[0][p], split[1][p], split[2][p]])
+            put_rows(gs[n], sub, 8 * p + 4, [split[3][p]])
+        along = y[0] * f[0] + y[1] * f[1] + y[2] * f[2]
+        line = [f[0], f[1], f[2], along]
+        values = list(line)
+        for i in range(3):
+            values += [y[i] * v for v in line]
+        values += [square * v for v in f]
+        for r, value in enumerate(values):
+            for p, piece in enumerate(pieces(value)):
+                put_rows(gc[n], sub, p * COEF + r, [piece])
     for k in range(sub):
-        h, m, l = [strided(gs_ref, p * 8 * sub + k, 8, sub) for p in range(3)]
-        block = jnp.concatenate([h, m, h, l, h, m], axis=0).T.astype(bf16)
-        side_ref[base + k * LANES : base + (k + 1) * LANES, :] = block
-        rows = strided(gc_ref, k, coef_ref.shape[0], sub)
-        coef_ref[:, base + k * LANES : base + (k + 1) * LANES] = rows.astype(bf16)
+        groups = []
+        for n in range(len(sources)):
+            h, m, l = [strided(gs[n], p * 8 * sub + k, 8, sub) for p in range(3)]
+            groups += [h, m, h, l, h, m]
+            rows = strided(gc[n], k, coef_ref.shape[0], sub)
+            at = n * points + k * LANES
+            coef_ref[:, at : at + LANES] = rows.astype(bf16)
+        block = jnp.concatenate(groups, axis=0).T.astype(bf16)
+        side_ref[k * LANES : (k + 1) * LANES, :] = block
+
+
+COEF = 19
 
 
 def finish(x, total):
@@ -129,27 +135,30 @@
     return out
 
 
-COEF = 19
-
-
 def mega_kernel(
     shape,
     listed,
     near_ref,
     drag_ref,
-    pos_ref,
+    pos_hbm,
     analysis_hbm,
-    stiffness_ref,
+    stiffness_hbm,
     synthesis_hbm,
-    wpos_ref,
-    wnormal_ref,
-    wweight_ref,
-    wdensity_ref,
+    wpos_hbm,
+    wnormal_hbm,
+    wweight_hbm,
+    wdensity_hbm,
     pnear_ref,
     cpatch_ref,
     speed_ref,
     top_ref,
     half_ref,
+    pos_ref,
+    stiffness_ref,
+    wpos_ref,
+    wnormal_ref,
+    wweight_ref,
+    wdensity_ref,
     analysis_ref,
     synthesis_ref,
     e_ref,
@@ -157,11 +166,17 @@
     v_ref,
     gs_a,
     gs_b,
+    gs_c,
+    gs_d,
     gc_a,
     gc_b,
+    gc_c,
+    gc_d,
     gt_ref,
     side_ref,
     coef_ref,
+    side_b,
+    coef_b,
     feats_ref,
     cube_a,
     cube_b,
@@ -204,14 +219,20 @@
     gs, gc, cubes = (gs_a, gs_b), (gc_a, gc_b), (cube_a, cube_b)
     size_x, size_y = shape.size_x, shape.size_y
     rows, cols, sub, cell = shape.rows, shape.cols, shape.sub, shape.cell
-    patches, wpoints = wpos_ref.shape[1], wpos_ref.shape[2]
+    patches, wpoints = wpos_hbm.shape[1], wpos_hbm.shape[2]
     wtiles = wpoints // LANES
 
     weights = [
         pltpu.make_async_copy(analysis_hbm, analysis_ref, local.at[0]),
         pltpu.make_async_copy(synthesis_hbm, synthesis_ref, local.at[1]),
+        pltpu.make_async_copy(stiffness_hbm, stiffness_ref, local.at[2]),
     ]
-    for copy in weights:
+    pairs = (
+        (pos_hbm, pos_ref), (wpos_hbm, wpos_ref), (wnormal_hbm, wnormal_ref),
+        (wweight_hbm, wweight_ref), (wdensity_hbm, wdensity_ref),
+    )
+    inputs = [pltpu.make_async_copy(src, dst, local.at[3 + k]) for k, (src, dst) in enumerate(pairs)]
+    for copy in inputs + weights:
         copy.start()
 
     def around(step_x, step_y):
@@ -230,18 +251,20 @@
     for device in greeted:
         pl.semaphore_signal(barrier, inc=1, device_id=device, device_id_type=MESH)
 
+    e_ref[shape.slots * cell :, :] = jnp.zeros_like(e_ref[shape.slots * cell :, :])
+    for ref in (*gs, gs_c, gs_d, *gc, gc_c, gc_d, gt_ref, gd_ref, gq_ref, gm_ref, gf_ref, gw_ref):
+        ref[...] = jnp.zeros_like(ref)
+    one = jnp.ones((sub, LANES), f32)
+    for ref in (*gs, gs_c, gs_d):
+        ref[3 * sub : 4 * sub, :] = one
+    gt_ref[4 * sub : 5 * sub, :] = one
+    for copy in inputs:
+        copy.wait()
     for r in range(rows):
         for c in range(cols):
             for i in range(3):
                 at = ((r * cols + c) * 3 + i) * sub
                 e_ref[at : at + sub, :] = strided(pos_ref, (r * 3 + i) * sub * cols + c, sub, cols)
-    e_ref[shape.slots * cell :, :] = jnp.zeros_like(e_ref[shape.slots * cell :, :])
-    for ref in (*gs, *gc, gt_ref, gd_ref, gq_ref, gm_ref, gf_ref, gw_ref):
-        ref[...] = jnp.zeros_like(ref)
-    one = jnp.ones((sub, LANES), f32)
-    for ref in gs:
-        ref[3 * sub : 4 * sub, :] = one
-    gt_ref[4 * sub : 5 * sub, :] = one
 
     pl.semaphore_wait(barrier, len(greeted))
 
@@ -290,9 +313,9 @@
             k = len(ws)
             ws.append(remote(src, dst.at[b], wsend.at[k], wrecv.at[k], device))
 
+    for copy in ws:
+        copy.start()
     for copy, _ in xs:
-        copy.start()
-    for copy in ws:
         copy.start()
     ys = []
     for row in range(rows):
@@ -310,7 +333,11 @@
         for k in range(sub):
             h, m, l = [strided(gt_ref, p * 8 * sub + k, 8, sub) for p in range(3)]
             tiles.append(jnp.concatenate([h, h, m, h, l, m], axis=0).astype(bf16))
-        feats_ref[i] = jnp.concatenate(tiles, axis=1)
+        first = (shape.near - 1) * 48
+        blank = jnp.zeros((first, shape.points), bf16)
+        feats_ref[i, :first, :] = blank
+        feats_ref[i, first : first + 48, :] = jnp.concatenate(tiles, axis=1)
+        feats_ref[i, first + 48 :, :] = blank
         return 0
 
     lax.fori_loop(0, rows * cols, target, 0)
@@ -328,9 +355,17 @@
             put_wide(gw_ref, (8 * p + r) * patches, piece)
     for q in range(patches):
         h, m, l = [get_wide(gf_ref, wtiles, p * 16 * patches + q, 16, patches) for p in range(3)]
-        lfeat_ref[q * 96 : (q + 1) * 96, :] = jnp.concatenate([h, h, m, h, l, m], axis=0).astype(bf16)
+        wide = jnp.concatenate([h, h, m, h, l, m], axis=0).astype(bf16)
+        blank = jnp.zeros_like(wide)
+        for k in range(2):
+            rows2 = [wide if j == k else blank for j in range(2)]
+            lfeat_ref[q, :, k * wpoints : (k + 1) * wpoints] = jnp.concatenate(rows2, axis=0)
         h, m, l = [get_wide(gw_ref, wtiles, p * 8 * patches + q, 8, patches) for p in range(3)]
-        wfeat_ref[q * 48 : (q + 1) * 48, :] = jnp.concatenate([h, h, m, h, l, m], axis=0).astype(bf16)
+        wide = jnp.concatenate([h, h, m, h, l, m], axis=0).astype(bf16)
+        blank = jnp.zeros_like(wide)
+        for k in range(shape.near):
+            rows2 = [wide if j == k else blank for j in range(shape.near)]
+            wfeat_ref[q, :, k * wpoints : (k + 1) * wpoints] = jnp.concatenate(rows2, axis=0)
 
     def wall_sources(b, y, n, v, w):
         w = -layer_scale * w
@@ -355,19 +390,20 @@
 
         def one_patch(q, _):
             slot = b * patches + q
-            for s, ref in enumerate((gd_ref, gq_ref)):
-                for k in range(wtiles):
+            for k in range(wtiles):
+                groups = []
+                for ref in (gd_ref, gq_ref):
                     h, m, l = [
                         get_tile(ref, wtiles, k, p * 16 * patches + q, 16, patches) for p in range(3)
                     ]
-                    block = jnp.concatenate([h, m, h, l, h, m], axis=0).T.astype(bf16)
-                    at = s * wpoints + k * LANES
-                    lside_ref[slot, at : at + LANES, :] = block
+                    groups += [h, m, h, l, h, m]
+                block = jnp.concatenate(groups, axis=0).T.astype(bf16)
+                lside_ref[slot, k * LANES : (k + 1) * LANES, :] = block
             rows16 = get_wide(gm_ref, wtiles, q, 16, patches)
             lmom_ref[slot] = rows16.astype(bf16)
             return 0
 
-        lax.fori_loop(0, patches, one_patch, 0)
+        lax.fori_loop(0, patches, one_patch, 0, unroll=2)
 
     wall_sources(
         1, x, [wnormal_ref[i] for i in range(3)], [wdensity_ref[i] for i in range(3)], wweight_ref[...]
@@ -415,33 +451,36 @@
             at = pl.multiple_of(k * height + t * value.shape[0], 8)
             ref[pl.ds(at, value.shape[0]), :] = value[:, k * LANES : (k + 1) * LANES]
 
-    def layer_patch(t, _):
-        feat = lfeat_ref[pl.ds(pl.multiple_of(t * 96, 16), 96), :]
-        total = None
-        for n in range(listed + 1):
-            if n == 0:
-                slot = t + patches
-            else:
-                slot = pnear_ref[n - 1, t] - block_start + patches
-                slot = jnp.where(slot < 0, slot + all_patches, slot)
-                slot = jnp.where(slot >= all_patches, slot - all_patches, slot)
-                slot = jnp.clip(slot, 0, 3 * patches - 1)
-            side = lside_ref[slot]
-            both = jnp.dot(side, feat, preferred_element_type=f32)
-            root = lax.rsqrt(both[:wpoints])
+    def layer_slot(t, n):
+        if n == 0:
+            return t + patches
+        slot = pnear_ref[n - 1, t] - block_start + patches
+        slot = jnp.where(slot < 0, slot + all_patches, slot)
+        slot = jnp.where(slot >= all_patches, slot - all_patches, slot)
+        return jnp.clip(slot, 0, 3 * patches - 1)
+
+    def layer_pair(j, _):
+        slots = [[layer_slot(2 * j + u, n) for n in range(listed + 1)] for u in range(2)]
+        scalars = []
+        for u in range(2):
+            side = jnp.concatenate([lside_ref[slot] for slot in slots[u]], axis=0)
+            both = jnp.dot(side, lfeat_ref[2 * j + u], preferred_element_type=f32)
+            root = lax.rsqrt(both[:, :wpoints])
             square = root * root
-            scalar = (both[wpoints:] * (square * square * root)).astype(bf16)
-            moment = lmom_ref[slot]
-            part = jnp.dot(moment, scalar, preferred_element_type=f32)
-            total = part if total is None else total + part
-        put_patch(lacc_ref, t, total)
+            scalars.append((both[:, wpoints:] * (square * square * root)).astype(bf16))
+        moment = jnp.concatenate(
+            [jnp.concatenate([lmom_ref[slot] for slot in slots[u]], axis=1) for u in range(2)], axis=0
+        )
+        total = jnp.dot(moment, jnp.concatenate(scalars, axis=1), preferred_element_type=f32)
+        for u in range(2):
+            put_patch(lacc_ref, 2 * j + u, total[16 * u : 16 * u + 16, u * wpoints : (u + 1) * wpoints])
         return 0
 
     done = 0
     for j in range(HALO):
         pass_on(xs[2 * j : 2 * j + 2])
-        upto = patches if j == HALO - 1 else (j + 1) * patches // 4
-        lax.fori_loop(done, upto, layer_patch, 0)
+        upto = patches // 2 if j == HALO - 1 else (j + 1) * patches // 8
+        lax.fori_loop(done, upto, layer_pair, 0)
         done = upto
 
     membrane(3 * rows * cols, 3 * 2 * HALO * cols)
@@ -449,19 +488,23 @@
         copy.wait_recv()
     membrane(3 * shape.left, -(-3 * (shape.slots - shape.left) // 8) * 8)
 
+    def prepare(gids, side_ref, coef_ref, gs, gc):
+        slots = [cell_slot(shape, gid, me_x, me_y) for gid in gids]
+        sources = [(cell_points(e_cells, k, shape), cell_points(f_cells, k, shape)) for k in slots]
+        prepare_sources(sources, side_ref, coef_ref, gs, gc, shape)
+
     def cell_prepare(i):
         r = lax.div(i, jnp.int32(cols))
         c = i - r * cols
+        gids = [near_ref[r, n, c] for n in range(shape.near)]
+        prepare(gids, side_ref, coef_ref, gs, gc)
+
+    chunks = shape.points // WIDTH
+    half = shape.near * 48
+    parts = []
+    for at in range(0, shape.points, WIDTH):
         for n in range(shape.near):
-            slot = cell_slot(shape, near_ref[r, n, c], me_x, me_y)
-            prepare_source(
-                cell_points(e_cells, slot, shape), cell_points(f_cells, slot, shape),
-                side_ref, coef_ref, gs[n], gc[n], n * shape.points, shape,
-            )
-
-    chunks = shape.points // WIDTH
-    sources = shape.near * shape.points
-    steps = [slice(at, at + WIDTH) for at in range(0, sources, WIDTH)]
+            parts.append((slice(at, at + WIDTH), n, slice(n * shape.points + at, n * shape.points + at + WIDTH)))
 
     def weigh(part, cube_ref):
         return jnp.dot(coef_ref[:, part], cube_ref[part, :], preferred_element_type=f32)
@@ -472,12 +515,12 @@
             h_ref[pl.ds(tile, acc.shape[0], stride=sub), :] = acc[:, k * LANES : (k + 1) * LANES]
 
     def cell_sums(i):
-        last = None
         for t in range(chunks):
-            feat = feats_ref[i, :, t * WIDTH : (t + 1) * WIDTH]
             acc = None
-            for part in steps:
-                root = lax.rsqrt(jnp.dot(side_ref[part, :], feat, preferred_element_type=f32))
+            for near_rows, n, part in parts:
+                first = (shape.near - 1 - n) * 48
+                feat = feats_ref[i, first : first + half, t * WIDTH : (t + 1) * WIDTH]
+                root = lax.rsqrt(jnp.dot(side_ref[near_rows, :], feat, preferred_element_type=f32))
                 cubes[t % 2][part, :] = (root * root * root).astype(bf16)
                 if t > 0:
                     more = weigh(part, cubes[(t - 1) % 2])
@@ -485,7 +528,7 @@
             if t > 0:
                 keep(t - 1, acc)
         acc = None
-        for part in steps:
+        for _, _, part in parts:
             more = weigh(part, cubes[(chunks - 1) % 2])
             acc = more if acc is None else acc + more
         keep(chunks - 1, acc)
@@ -520,25 +563,39 @@
     best = lax.fori_loop(0, rows * cols, cell_step, jnp.zeros((sub, LANES), f32))
     mine_ref[...] = best
 
-    def wall_prepare(t):
-        for n in range(cpatch_ref.shape[0]):
-            slot = cell_slot(shape, cpatch_ref[n, t], me_x, me_y)
-            prepare_source(
-                cell_points(e_cells, slot, shape), cell_points(f_cells, slot, shape),
-                side_ref, coef_ref, gs[n], gc[n], n * shape.points, shape,
-            )
-
-    def wall_step(t, _):
-        feat = wfeat_ref[pl.ds(pl.multiple_of(t * 48, 16), 48), :]
-        acc = None
-        for n in range(cpatch_ref.shape[0]):
-            part = slice(n * shape.points, (n + 1) * shape.points)
-            root = lax.rsqrt(jnp.dot(side_ref[part, :], feat, preferred_element_type=f32))
-            cube = (root * root * root).astype(bf16)
-            more = jnp.dot(coef_ref[:, part], cube, preferred_element_type=f32)
-            acc = more if acc is None else acc + more
-        put_patch(wacc_ref, t, acc)
-        wall_prepare(jnp.minimum(t + 1, patches - 1))
+    sets = ((side_ref, coef_ref, gs, gc), (side_b, coef_b, (gs_c, gs_d), (gc_c, gc_d)))
+
+    def wall_prepare(j):
+        for u in range(2):
+            gids = [cpatch_ref[n, 2 * j + u] for n in range(shape.near)]
+            prepare(gids, *sets[u])
+
+    def wall_pair(j, _):
+        accs = [None, None]
+        for at in range(0, shape.points, WIDTH):
+            cubes2 = []
+            for u in range(2):
+                square = jnp.dot(
+                    sets[u][0][at : at + WIDTH, :], wfeat_ref[2 * j + u], preferred_element_type=f32
+                )
+                root = lax.rsqrt(square)
+                cubes2.append((root * root * root).astype(bf16))
+            for u in range(2):
+                coef = sets[u][1]
+                both = jnp.concatenate(
+                    [coef[:, n * shape.points + at : n * shape.points + at + WIDTH] for n in range(shape.near)],
+                    axis=0,
+                )
+                more = jnp.dot(both, cubes2[u], preferred_element_type=f32)
+                accs[u] = more if accs[u] is None else accs[u] + more
+        count = coef_ref.shape[0]
+        for u in range(2):
+            blocks = [
+                accs[u][n * count : (n + 1) * count, n * wpoints : (n + 1) * wpoints]
+                for n in range(shape.near)
+            ]
+            put_patch(wacc_ref, 2 * j + u, functools.reduce(jnp.add, blocks))
+        wall_prepare(jnp.minimum(j + 1, patches // 2 - 1))
         return 0
 
     wall_prepare(jnp.int32(0))
@@ -546,18 +603,20 @@
     for d, device in enumerate(peers_y):
         copies.append(remote(mine_ref, from_y.at[d], tsend_y.at[d], trecv_y.at[d], device))
         copies[-1].start()
-    half = patches // 2 - 1
-    lax.fori_loop(0, half, wall_step, 0)
+    lax.fori_loop(0, 1, wall_pair, 0)
     best = mine_ref[...]
     for d, copy in enumerate(copies):
         copy.wait_recv()
         best = jnp.maximum(best, from_y[d])
     row_ref[...] = best
-    lax.fori_loop(half, half + 1, wall_step, 0)
+    moment = [get_wide(lacc_ref, wtiles, r, patches, 16) for r in range(11)]
+    moment = [moment[i] + (moment[4 + i] + moment[8 + i]) for i in range(3)] + [moment[3]]
+    for i in range(3):
+        half_ref[i] = x[i] * moment[3] - moment[i]
     for d, device in enumerate(peers_x):
         copies.append(remote(row_ref, from_x.at[d], tsend_x.at[d], trecv_x.at[d], device))
         copies[-1].start()
-    lax.fori_loop(half + 1, patches, wall_step, 0)
+    lax.fori_loop(1, patches // 2, wall_pair, 0)
 
     def wall_total(row):
         a, b, d = [
@@ -566,11 +625,8 @@
         return a + (b + d)
 
     flow = finish(x, wall_total)
-    moment = [get_wide(lacc_ref, wtiles, r, patches, 16) for r in range(11)]
-    moment = [moment[i] + (moment[4 + i] + moment[8 + i]) for i in range(3)] + [moment[3]]
     for i in range(3):
-        layer = x[i] * moment[3] - moment[i]
-        half_ref[i] = layer + flow[i]
+        half_ref[i] = half_ref[i] + flow[i]
 
     best = row_ref[...]
     for d, copy in enumerate(copies[size_y - 1 :]):
@@ -621,13 +677,13 @@
     wtiles = wpoints // LANES
     spare = -(-shape.slots // 8) * 8
     sources = near * points
-    assert cell_to_patch.shape[1] == near
+    assert cell_to_patch.shape[1] == near and patches % 2 == 0
     coef_rows = -(-3 * COEF // 16) * 16
     dma = pltpu.SemaphoreType.DMA
     vmem = pltpu.VMEM
     in_vmem = pl.BlockSpec(memory_space=pltpu.VMEM)
     in_smem = pl.BlockSpec(memory_space=pltpu.SMEM)
-    in_hbm = pl.BlockSpec(memory_space=pl.ANY)
+    in_hbm = pl.BlockSpec(memory_space=pltpu.HBM)
     walls = lambda v: jnp.transpose(v, (1, 0, 2))
     speed, top, half = pl.pallas_call(
         functools.partial(mega_kernel, shape, listed),
@@ -637,11 +693,17 @@
             jax.ShapeDtypeStruct((3, patches, wpoints), f32),
         ),
         in_specs=[
-            in_smem, in_smem, in_vmem, in_hbm, in_vmem, in_hbm,
-            in_vmem, in_vmem, in_vmem, in_vmem, in_smem, in_smem,
+            in_smem, in_smem, in_hbm, in_hbm, in_hbm, in_hbm,
+            in_hbm, in_hbm, in_hbm, in_hbm, in_smem, in_smem,
         ],
         out_specs=[in_vmem] * 3,
         scratch_shapes=[
+            vmem(raw.shape, f32),
+            vmem((1, stiffness.shape[0]), f32),
+            vmem((3, patches, wpoints), f32),
+            vmem((3, patches, wpoints), f32),
+            vmem((patches, wpoints), f32),
+            vmem((3, patches, wpoints), f32),
             vmem(analysis.shape, bf16),
             vmem(synthesis.shape, bf16),
             vmem((spare, cell, LANES), f32),
@@ -649,12 +711,18 @@
             vmem((rows * cols * cell, LANES), f32),
             vmem((24 * sub, LANES), f32),
             vmem((24 * sub, LANES), f32),
+            vmem((24 * sub, LANES), f32),
+            vmem((24 * sub, LANES), f32),
+            vmem((coef_rows * sub, LANES), f32),
+            vmem((coef_rows * sub, LANES), f32),
             vmem((coef_rows * sub, LANES), f32),
             vmem((coef_rows * sub, LANES), f32),
             vmem((24 * sub, LANES), f32),
-            vmem((sources, 48), bf16),
+            vmem((points, near * 48), bf16),
             vmem((coef_rows, sources), bf16),
-            vmem((rows * cols, 48, points), bf16),
+            vmem((points, near * 48), bf16),
+            vmem((coef_rows, sources), bf16),
+            vmem((rows * cols, (2 * near - 1) * 48, points), bf16),
             vmem((sources, WIDTH), bf16),
             vmem((sources, WIDTH), bf16),
             vmem((coef_rows * sub, LANES), f32),
@@ -667,17 +735,17 @@
             vmem((16 * patches * wtiles, LANES), f32),
             vmem((48 * patches * wtiles, LANES), f32),
             vmem((24 * patches * wtiles, LANES), f32),
-            vmem((3 * patches, 2 * wpoints, 96), bf16),
+            vmem((3 * patches, wpoints, 192), bf16),
             vmem((3 * patches, 16, wpoints), bf16),
-            vmem((patches * 96, wpoints), bf16),
-            vmem((patches * 48, wpoints), bf16),
+            vmem((patches, 192, 2 * wpoints), bf16),
+            vmem((patches, near * 48, near * wpoints), bf16),
             vmem((patches * 16 * wtiles, LANES), f32),
             vmem((patches * coef_rows * wtiles, LANES), f32),
             vmem((sub, LANES), f32),
             vmem((sub, LANES), f32),
             vmem((size_y - 1, sub, LANES), f32),
             vmem((size_x - 1, sub, LANES), f32),
-            dma((2,)),
+            dma((8,)),
             dma((2 * HALO,)),
             dma((2 * HALO,)),
             dma((2 * shape.ext_rows,)),

time: 71.5 us -> 66 us (0.923)
  Pallas kernels: 70.7 us -> 65.1 us
    pallas_call x1, Pallas kernels: 68.8 us -> 63.3 us  [body(): pl.pallas_call(functools.partial(mega_kernel, shape, listed), out_shape=(...]
where the time goes in v3:
time: 66 us; the launch traced here: 65.8 us
  Pallas kernels  65.1 us (99%)
    pallas_call x1, Pallas kernels, body(): pl.pallas_call(functools.partial(mega_kernel, shape, listed), out_shape=(...  63.3 us
    pallas_call x1, Pallas kernels, body(): pl.pallas_call(update_kernel, out_shape=(jax.ShapeDtypeStruct(raw.shape,...  1.86 us

profile of v3, /device:TPU:0, one launch (start us, length us, event | category | flops | bytes accessed | tf_op | source)
XLA Modules:
  0.0 65.8 jit_solution(17511481187278886303)
XLA Ops:
  0.6 63.3 %mega.1 = (f32[384,128]{1,0:T(8,128)}, f32[8,128]{1,0:T(8,128)}, f32[3,8,256]{2,1,0:T(8,128)}) custom-call(s32[4,2,4]{2,1,0:T(2,128)} %bitcast.23, f32[4,4]{1,0:T(4,128)} %drag_ref.1, f32[384,128]{1,0:T(8,128)} %bitcast.18, bf16[1024,1024]{1,0:T(8,128)(2,1)} %analysis_hbm.1, f32[1,1024]{1,0:T(1,128)} %bitcast.24, bf16[1024,1024]{1,0:T(8,128)(2,1)} %synthesis_hbm.1, ...), custom_call_target="tpu_custom_call" | custom-call | tf_op jit(solution)/shard_map/mega/pallas_call | solution.py:688
  63.9 1.9 %update.1 = (f32[384,128]{1,0:T(8,128)}, f32[3,8,256]{2,1,0:T(8,128)}) custom-call(f32[384,128]{1,0:T(8,128)} %bitcast.19, f32[384,128]{1,0:T(8,128)} %get-tuple-element.7.speed_ref, f32[8,128]{1,0:T(8,128)} %get-tuple-element.8.top_ref, f32[3,8,256]{2,1,0:T(8,128)} %get-tuple-element.9.half_ref), custom_call_target="tpu_custom_call" | custom-call | tf_op jit(solution)/shard_map/update/pallas_call | solution.py:778

commit v4 on v3

--- a/solution.py
+++ b/solution.py
@@ -424,17 +424,6 @@
 
     membrane(0, 3 * rows * cols)
 
-    for copy in ws:
-        copy.wait_recv()
-    for b in range(2):
-        wall_sources(
-            2 * b,
-            [hp_ref[b, i] for i in range(3)],
-            [hn_ref[b, i] for i in range(3)],
-            [hd_ref[b, i] for i in range(3)],
-            hw_ref[b],
-        )
-
     def pass_on(pairs):
         for copy, row in pairs:
             copy.wait_recv()
@@ -476,12 +465,34 @@
             put_patch(lacc_ref, 2 * j + u, total[16 * u : 16 * u + 16, u * wpoints : (u + 1) * wpoints])
         return 0
 
-    done = 0
-    for j in range(HALO):
-        pass_on(xs[2 * j : 2 * j + 2])
-        upto = patches // 2 if j == HALO - 1 else (j + 1) * patches // 8
-        lax.fori_loop(done, upto, layer_pair, 0)
-        done = upto
+    pass_on(xs[:1])
+    for copy in ws:
+        copy.wait_recv()
+    for b in range(1):
+        wall_sources(
+            2 * b,
+            [hp_ref[b, i] for i in range(3)],
+            [hn_ref[b, i] for i in range(3)],
+            [hd_ref[b, i] for i in range(3)],
+            hw_ref[b],
+        )
+
+    pass_on(xs[1:2])
+    for b in range(1, 2):
+        wall_sources(
+            2 * b,
+            [hp_ref[b, i] for i in range(3)],
+            [hn_ref[b, i] for i in range(3)],
+            [hd_ref[b, i] for i in range(3)],
+            hw_ref[b],
+        )
+
+    pass_on(xs[2:4])
+    lax.fori_loop(0, 1, layer_pair, 0)
+    pass_on(xs[4:5])
+    lax.fori_loop(1, 2, layer_pair, 0)
+    pass_on(xs[5:])
+    lax.fori_loop(2, patches // 2, layer_pair, 0)
 
     membrane(3 * rows * cols, 3 * 2 * HALO * cols)
     for copy in ys:
@@ -502,9 +513,8 @@
     chunks = shape.points // WIDTH
     half = shape.near * 48
     parts = []
-    for at in range(0, shape.points, WIDTH):
-        for n in range(shape.near):
-            parts.append((slice(at, at + WIDTH), n, slice(n * shape.points + at, n * shape.points + at + WIDTH)))
+    for n in range(shape.near):
+        parts.append((slice(0, shape.points), n, slice(n * shape.points, (n + 1) * shape.points)))
 
     def weigh(part, cube_ref):
         return jnp.dot(coef_ref[:, part], cube_ref[part, :], preferred_element_type=f32)

time: 66 us -> 65.4 us (level)
  no operation moved by 1% of the time
where the time goes in v4:
time: 65.4 us; the launch traced here: 65.3 us
  Pallas kernels  64.6 us (99%)
    pallas_call x1, Pallas kernels, body(): pl.pallas_call(functools.partial(mega_kernel, shape, listed), out_shape=(...  62.8 us
    pallas_call x1, Pallas kernels, body(): pl.pallas_call(update_kernel, out_shape=(jax.ShapeDtypeStruct(raw.shape,...  1.86 us

profile of v4, /device:TPU:0, one launch (start us, length us, event | category | flops | bytes accessed | tf_op | source)
XLA Modules:
  0.0 65.3 jit_solution(15744772351532164066)
XLA Ops:
  0.6 62.8 %mega.1 = (f32[384,128]{1,0:T(8,128)}, f32[8,128]{1,0:T(8,128)}, f32[3,8,256]{2,1,0:T(8,128)}) custom-call(s32[4,2,4]{2,1,0:T(2,128)} %bitcast.23, f32[4,4]{1,0:T(4,128)} %drag_ref.1, f32[384,128]{1,0:T(8,128)} %bitcast.18, bf16[1024,1024]{1,0:T(8,128)(2,1)} %analysis_hbm.1, f32[1,1024]{1,0:T(1,128)} %bitcast.24, bf16[1024,1024]{1,0:T(8,128)(2,1)} %synthesis_hbm.1, ...), custom_call_target="tpu_custom_call" | custom-call | tf_op jit(solution)/shard_map/mega/pallas_call | solution.py:698
  63.4 1.9 %update.1 = (f32[384,128]{1,0:T(8,128)}, f32[3,8,256]{2,1,0:T(8,128)}) custom-call(f32[384,128]{1,0:T(8,128)} %bitcast.19, f32[384,128]{1,0:T(8,128)} %get-tuple-element.7.speed_ref, f32[8,128]{1,0:T(8,128)} %get-tuple-element.8.top_ref, f32[3,8,256]{2,1,0:T(8,128)} %get-tuple-element.9.half_ref), custom_call_target="tpu_custom_call" | custom-call | tf_op jit(solution)/shard_map/update/pallas_call | solution.py:788

commit v5 on v4

--- a/solution.py
+++ b/solution.py
@@ -88,7 +88,7 @@
         ref[(first + i) * sub : (first + i + 1) * sub, :] = value
 
 
-def prepare_sources(sources, side_ref, coef_ref, gs, gc, shape):
+def prepare_sources(sources, side_ref, coef_ref, gs, gc, shape, apart):
     sub, points = shape.sub, shape.points
     for n, (y, f) in enumerate(sources):
         square = y[0] * y[0] + y[1] * y[1] + y[2] * y[2]
@@ -113,8 +113,13 @@
             rows = strided(gc[n], k, coef_ref.shape[0], sub)
             at = n * points + k * LANES
             coef_ref[:, at : at + LANES] = rows.astype(bf16)
-        block = jnp.concatenate(groups, axis=0).T.astype(bf16)
-        side_ref[k * LANES : (k + 1) * LANES, :] = block
+            if apart:
+                at = n * points + k * LANES
+                side_ref[at : at + LANES, :] = jnp.concatenate(groups, axis=0).T.astype(bf16)
+                groups = []
+        if not apart:
+            block = jnp.concatenate(groups, axis=0).T.astype(bf16)
+            side_ref[k * LANES : (k + 1) * LANES, :] = block
 
 
 COEF = 19
@@ -150,9 +155,10 @@
     wdensity_hbm,
     pnear_ref,
     cpatch_ref,
-    speed_ref,
+    speed_hbm,
     top_ref,
     half_ref,
+    speed_ref,
     pos_ref,
     stiffness_ref,
     wpos_ref,
@@ -174,6 +180,7 @@
     gc_d,
     gt_ref,
     side_ref,
+    cside_ref,
     coef_ref,
     side_b,
     coef_b,
@@ -333,11 +340,7 @@
         for k in range(sub):
             h, m, l = [strided(gt_ref, p * 8 * sub + k, 8, sub) for p in range(3)]
             tiles.append(jnp.concatenate([h, h, m, h, l, m], axis=0).astype(bf16))
-        first = (shape.near - 1) * 48
-        blank = jnp.zeros((first, shape.points), bf16)
-        feats_ref[i, :first, :] = blank
-        feats_ref[i, first : first + 48, :] = jnp.concatenate(tiles, axis=1)
-        feats_ref[i, first + 48 :, :] = blank
+        feats_ref[i] = jnp.concatenate(tiles, axis=1)
         return 0
 
     lax.fori_loop(0, rows * cols, target, 0)
@@ -494,27 +497,26 @@
     pass_on(xs[5:])
     lax.fori_loop(2, patches // 2, layer_pair, 0)
 
-    membrane(3 * rows * cols, 3 * 2 * HALO * cols)
     for copy in ys:
         copy.wait_recv()
-    membrane(3 * shape.left, -(-3 * (shape.slots - shape.left) // 8) * 8)
-
-    def prepare(gids, side_ref, coef_ref, gs, gc):
+    membrane(3 * rows * cols, -(-3 * (shape.slots - rows * cols) // 8) * 8)
+
+    def prepare(gids, side_ref, coef_ref, gs, gc, apart=False):
         slots = [cell_slot(shape, gid, me_x, me_y) for gid in gids]
         sources = [(cell_points(e_cells, k, shape), cell_points(f_cells, k, shape)) for k in slots]
-        prepare_sources(sources, side_ref, coef_ref, gs, gc, shape)
+        prepare_sources(sources, side_ref, coef_ref, gs, gc, shape, apart)
 
     def cell_prepare(i):
         r = lax.div(i, jnp.int32(cols))
         c = i - r * cols
         gids = [near_ref[r, n, c] for n in range(shape.near)]
-        prepare(gids, side_ref, coef_ref, gs, gc)
+        prepare(gids, cside_ref, coef_ref, gs, gc, True)
 
     chunks = shape.points // WIDTH
     half = shape.near * 48
     parts = []
     for n in range(shape.near):
-        parts.append((slice(0, shape.points), n, slice(n * shape.points, (n + 1) * shape.points)))
+        parts.append((None, n, slice(n * shape.points, (n + 1) * shape.points)))
 
     def weigh(part, cube_ref):
         return jnp.dot(coef_ref[:, part], cube_ref[part, :], preferred_element_type=f32)
@@ -528,9 +530,8 @@
         for t in range(chunks):
             acc = None
             for near_rows, n, part in parts:
-                first = (shape.near - 1 - n) * 48
-                feat = feats_ref[i, first : first + half, t * WIDTH : (t + 1) * WIDTH]
-                root = lax.rsqrt(jnp.dot(side_ref[near_rows, :], feat, preferred_element_type=f32))
+                feat = feats_ref[i, :, t * WIDTH : (t + 1) * WIDTH]
+                root = lax.rsqrt(jnp.dot(cside_ref[part, :], feat, preferred_element_type=f32))
                 cubes[t % 2][part, :] = (root * root * root).astype(bf16)
                 if t > 0:
                     more = weigh(part, cubes[(t - 1) % 2])
@@ -608,12 +609,19 @@
         wall_prepare(jnp.minimum(j + 1, patches // 2 - 1))
         return 0
 
+    for r in range(rows):
+        for c in range(cols):
+            for i in range(3):
+                at = ((r * cols + c) * 3 + i) * sub
+                speed_ref[pl.ds((r * 3 + i) * sub * cols + c, sub, stride=cols), :] = v_ref[at : at + sub, :]
     wall_prepare(jnp.int32(0))
     copies = []
     for d, device in enumerate(peers_y):
         copies.append(remote(mine_ref, from_y.at[d], tsend_y.at[d], trecv_y.at[d], device))
         copies[-1].start()
     lax.fori_loop(0, 1, wall_pair, 0)
+    speeds = pltpu.make_async_copy(speed_ref, speed_hbm, local.at[8])
+    speeds.start()
     best = mine_ref[...]
     for d, copy in enumerate(copies):
         copy.wait_recv()
@@ -643,11 +651,7 @@
         copy.wait_recv()
         best = jnp.maximum(best, from_x[d])
     top_ref[...] = best
-    for r in range(rows):
-        for c in range(cols):
-            for i in range(3):
-                at = ((r * cols + c) * 3 + i) * sub
-                speed_ref[pl.ds((r * 3 + i) * sub * cols + c, sub, stride=cols), :] = v_ref[at : at + sub, :]
+    speeds.wait()
     for copy, _ in xs:
         copy.wait_send()
     for copy in ws + ys + copies:
@@ -706,8 +710,9 @@
             in_smem, in_smem, in_hbm, in_hbm, in_hbm, in_hbm,
             in_hbm, in_hbm, in_hbm, in_hbm, in_smem, in_smem,
         ],
-        out_specs=[in_vmem] * 3,
+        out_specs=[in_hbm, in_vmem, in_vmem],
         scratch_shapes=[
+            vmem(raw.shape, f32),
             vmem(raw.shape, f32),
             vmem((1, stiffness.shape[0]), f32),
             vmem((3, patches, wpoints), f32),
@@ -729,10 +734,11 @@
             vmem((coef_rows * sub, LANES), f32),
             vmem((24 * sub, LANES), f32),
             vmem((points, near * 48), bf16),
+            vmem((sources, 48), bf16),
             vmem((coef_rows, sources), bf16),
             vmem((points, near * 48), bf16),
             vmem((coef_rows, sources), bf16),
-            vmem((rows * cols, (2 * near - 1) * 48, points), bf16),
+            vmem((rows * cols, 48, points), bf16),
             vmem((sources, WIDTH), bf16),
             vmem((sources, WIDTH), bf16),
             vmem((coef_rows * sub, LANES), f32),
@@ -755,7 +761,7 @@
             vmem((sub, LANES), f32),
             vmem((size_y - 1, sub, LANES), f32),
             vmem((size_x - 1, sub, LANES), f32),
-            dma((8,)),
+            dma((9,)),
             dma((2 * HALO,)),
             dma((2 * HALO,)),
             dma((2 * shape.ext_rows,)),

time: 65.4 us -> 64.8 us (level)
    pallas_call x1, Pallas kernels: 62.8 us -> 62.1 us  [body(): pl.pallas_call(functools.partial(mega_kernel, shape, listed), out_shape=(...]
where the time goes in v5:
time: 64.8 us; the launch traced here: 64.6 us
  Pallas kernels  64 us (99%)
    pallas_call x1, Pallas kernels, body(): pl.pallas_call(functools.partial(mega_kernel, shape, listed), out_shape=(...  62.1 us
    pallas_call x1, Pallas kernels, body(): pl.pallas_call(update_kernel, out_shape=(jax.ShapeDtypeStruct(raw.shape,...  1.86 us

profile of v5, /device:TPU:0, one launch (start us, length us, event | category | flops | bytes accessed | tf_op | source)
XLA Modules:
  0.0 64.6 jit_solution(398081111341317715)
XLA Ops:
  0.6 62.1 %mega.1 = (f32[384,128]{1,0:T(8,128)}, f32[8,128]{1,0:T(8,128)}, f32[3,8,256]{2,1,0:T(8,128)}) custom-call(s32[4,2,4]{2,1,0:T(2,128)} %bitcast.23, f32[4,4]{1,0:T(4,128)} %drag_ref.1, f32[384,128]{1,0:T(8,128)} %bitcast.18, bf16[1024,1024]{1,0:T(8,128)(2,1)} %analysis_hbm.1, f32[1,1024]{1,0:T(1,128)} %bitcast.24, bf16[1024,1024]{1,0:T(8,128)(2,1)} %synthesis_hbm.1, ...), custom_call_target="tpu_custom_call" | custom-call | tf_op jit(solution)/shard_map/mega/pallas_call | solution.py:702
  62.7 1.9 %update.1 = (f32[384,128]{1,0:T(8,128)}, f32[3,8,256]{2,1,0:T(8,128)}) custom-call(f32[384,128]{1,0:T(8,128)} %bitcast.19, f32[384,128]{1,0:T(8,128)} %get-tuple-element.7.speed_ref, f32[8,128]{1,0:T(8,128)} %get-tuple-element.8.top_ref, f32[3,8,256]{2,1,0:T(8,128)} %get-tuple-element.9.half_ref), custom_call_target="tpu_custom_call" | custom-call | tf_op jit(solution)/shard_map/update/pallas_call | solution.py:794

commit v6 on v5

--- a/solution.py
+++ b/solution.py
@@ -582,23 +582,17 @@
             prepare(gids, *sets[u])
 
     def wall_pair(j, _):
-        accs = [None, None]
-        for at in range(0, shape.points, WIDTH):
-            cubes2 = []
-            for u in range(2):
-                square = jnp.dot(
-                    sets[u][0][at : at + WIDTH, :], wfeat_ref[2 * j + u], preferred_element_type=f32
-                )
-                root = lax.rsqrt(square)
-                cubes2.append((root * root * root).astype(bf16))
-            for u in range(2):
-                coef = sets[u][1]
-                both = jnp.concatenate(
-                    [coef[:, n * shape.points + at : n * shape.points + at + WIDTH] for n in range(shape.near)],
-                    axis=0,
-                )
-                more = jnp.dot(both, cubes2[u], preferred_element_type=f32)
-                accs[u] = more if accs[u] is None else accs[u] + more
+        accs, cubes2 = [], []
+        for u in range(2):
+            square = jnp.dot(sets[u][0][...], wfeat_ref[2 * j + u], preferred_element_type=f32)
+            root = lax.rsqrt(square)
+            cubes2.append((root * root * root).astype(bf16))
+        for u in range(2):
+            coef = sets[u][1]
+            both = jnp.concatenate(
+                [coef[:, n * shape.points : (n + 1) * shape.points] for n in range(shape.near)], axis=0
+            )
+            accs.append(jnp.dot(both, cubes2[u], preferred_element_type=f32))
         count = coef_ref.shape[0]
         for u in range(2):
             blocks = [

time: 64.8 us -> 64.8 us (level)
  no operation moved by 1% of the time
where the time goes in v6:
time: 64.8 us; the launch traced here: 64.7 us
  Pallas kernels  64 us (99%)
    pallas_call x1, Pallas kernels, body(): pl.pallas_call(functools.partial(mega_kernel, shape, listed), out_shape=(...  62.2 us
    pallas_call x1, Pallas kernels, body(): pl.pallas_call(update_kernel, out_shape=(jax.ShapeDtypeStruct(raw.shape,...  1.86 us

profile of v6, /device:TPU:0, one launch (start us, length us, event | category | flops | bytes accessed | tf_op | source)
XLA Modules:
  0.0 64.7 jit_solution(6547336213128408266)
XLA Ops:
  0.6 62.2 %mega.1 = (f32[384,128]{1,0:T(8,128)}, f32[8,128]{1,0:T(8,128)}, f32[3,8,256]{2,1,0:T(8,128)}) custom-call(s32[4,2,4]{2,1,0:T(2,128)} %bitcast.23, f32[4,4]{1,0:T(4,128)} %drag_ref.1, f32[384,128]{1,0:T(8,128)} %bitcast.18, bf16[1024,1024]{1,0:T(8,128)(2,1)} %analysis_hbm.1, f32[1,1024]{1,0:T(1,128)} %bitcast.24, bf16[1024,1024]{1,0:T(8,128)(2,1)} %synthesis_hbm.1, ...), custom_call_target="tpu_custom_call" | custom-call | tf_op jit(solution)/shard_map/mega/pallas_call | solution.py:696
  62.8 1.9 %update.1 = (f32[384,128]{1,0:T(8,128)}, f32[3,8,256]{2,1,0:T(8,128)}) custom-call(f32[384,128]{1,0:T(8,128)} %bitcast.19, f32[384,128]{1,0:T(8,128)} %get-tuple-element.7.speed_ref, f32[8,128]{1,0:T(8,128)} %get-tuple-element.8.top_ref, f32[3,8,256]{2,1,0:T(8,128)} %get-tuple-element.9.half_ref), custom_call_target="tpu_custom_call" | custom-call | tf_op jit(solution)/shard_map/update/pallas_call | solution.py:788
